TPU v7x, 32 devices: a whole 2x2x4 slice. The times are simulated.
32 devices in a mesh: space: 8 (over z, x), chan: 4 (over y, core).
Axes of the slice: x: 2, y: 2, z: 4, core: 2. Of those that a mesh axis runs over, the one named last changes fastest.
Arguments:
- features: bfloat16 [512, 32, 512], P(('space', 'chan')), may hold values from -6 to 6
- occupancy: int32 [512], P(('space', 'chan')), may hold values 0 or 1
- neighbours: int32 [512, 6], P(('space', 'chan')), may hold values from -1 to 511, as said below
- conv_weight: bfloat16 [27, 32, 32], replicated, may hold values from -0.21875 to 0.21875
- conv_bias: float32 [32], replicated, may hold values from -3 to 3
- latent: bfloat16 [32768, 512], P(('space', 'chan')), may hold values from -6 to 6
- token_proj: bfloat16 [32, 512], replicated, may hold values from -1 to 1
- norm_gain: float32 [512], replicated, may hold values from 0.25 to 1.75
- qkv_weight: bfloat16 [3, 512, 512], replicated
- out_weight: bfloat16 [512, 512], replicated, may hold values from -0.25 to 0.25
Outputs:
- conv_out: bfloat16 [512, 32, 512], P(('space', 'chan'))
- tokens_out: bfloat16 [512, 32768], P(None, ('space', 'chan'))
Inputs may be any that keep to these rules, and one draw needn't show every extreme that they name: `neighbours`: entry [b, d] is the brick across face d of brick b (d = 0..5 for -x, +x, -y, +y, -z, +z), or -1 where there is none. Brick b lies on device b // 16 in the order of space+chan, and a neighbour lies on a device whose index differs from its brick's by at most 2.
All inputs are finite; a program needn't handle non-finite values. No bound on the sum of `occupancy` on one device may be relied on, other than what follows from the above.
Results may differ from a plain program's by a relative error of at most 0.0054.
Values may be sent and summed in bfloat16 or wider, within the bound.
No kernel may reach another device: no remote copies, remote signals or barrier semaphores. Data moves between devices by JAX's collectives and lax.ppermute only.
A program may use at most 128 MiB of HBM per device.

v0:
```python
import math

import jax
import jax.numpy as jnp
import numpy as np
from jax import lax
from jax.sharding import PartitionSpec as P

HD = 64
WIN = 1024
REACH = 2


def passed_along(value, axis, steps):
    count = lax.axis_size(axis)
    first, last = (max(0, -steps), min(count, count - steps))
    return lax.ppermute(value, axis, [(source, source + steps) for source in range(first, last)])


def shifted(array, axis, by):
    size = lax.axis_size(axis)
    return lax.ppermute(array, axis, [(i, (i + by) % size) for i in range(size)])


def sheet_sources():
    table = np.zeros((6, 64), np.int64)
    cells = np.arange(64)
    high, low = (cells // 8, cells % 8)
    table[0] = 448 + cells
    table[1] = cells
    table[2] = 64 * high + 56 + low
    table[3] = 64 * high + low
    table[4] = 64 * high + 8 * low + 7
    table[5] = 64 * high + 8 * low
    return table


def take_table():
    sources = sheet_sources()
    table = np.zeros((512, 6, 64), np.float32)
    for face in range(6):
        table[sources[face], face, np.arange(64)] = 1.0
    return jnp.asarray(table, jnp.bfloat16)


def place_table():
    sources = sheet_sources()
    table = np.zeros((6, 64, 512), np.float32)
    for face in range(6):
        table[face, np.arange(64), sources[face ^ 1]] = 1.0
    return jnp.asarray(table.reshape(3, 2, 64, 512), jnp.bfloat16)


def pool_table():
    table = np.zeros((512, 64), np.float32)
    for voxel in range(512):
        pos_x, pos_y, pos_z = (voxel // 64, voxel // 8 % 8, voxel % 8)
        cell_p, cell_q, cell_r = (pos_x // 2, pos_y // 2, pos_z // 2)
        target = (
            32 * (cell_p // 2)
            + 16 * (cell_q // 2)
            + 8 * (cell_r // 2)
            + 4 * (cell_p % 2)
            + 2 * (cell_q % 2)
            + cell_r % 2
        )
        table[voxel, target] = 0.125
    return jnp.asarray(table, jnp.bfloat16)


def shift_lanes(source, offset):
    if offset == 0:
        return source
    zero_shape = source.shape[:-1] + (abs(offset),)
    filler = jnp.zeros(zero_shape, source.dtype)
    if offset > 0:
        return jnp.concatenate([source[..., offset:], filler], axis=-1)
    return jnp.concatenate([filler, source[..., :offset]], axis=-1)


def inside(coord, step):
    return (coord + step >= 0) & (coord + step < 8)


def tap_inputs(vox, ghosts):
    lanes = jnp.arange(512, dtype=jnp.int32)
    coords = (lanes // 64, lanes // 8 % 8, lanes % 8)
    strides = (64, 8, 1)
    tap_list = []
    for step_x in (-1, 0, 1):
        for step_y in (-1, 0, 1):
            for step_z in (-1, 0, 1):
                steps_now = (step_x, step_y, step_z)
                offset = 64 * step_x + 8 * step_y + step_z
                within = (
                    inside(coords[0], step_x)
                    & inside(coords[1], step_y)
                    & inside(coords[2], step_z)
                )
                total = shift_lanes(vox, offset) * within.astype(vox.dtype)
                for axis_id in range(3):
                    if steps_now[axis_id] != 0:
                        others = [
                            inside(coords[other], steps_now[other])
                            for other in range(3)
                            if other != axis_id
                        ]
                        outside = (
                            jnp.logical_not(inside(coords[axis_id], steps_now[axis_id]))
                            & others[0]
                            & others[1]
                        )
                        ghost_shift = shift_lanes(
                            ghosts[:, axis_id], offset - steps_now[axis_id] * strides[axis_id]
                        )
                        total = total + ghost_shift * outside.astype(vox.dtype)
                tap_list.append(total)
    return jnp.stack(tap_list, axis=1)


def convolve(vox, ghosts, weight):
    brick_count, channels = (vox.shape[0], vox.shape[1])
    out_channels = weight.shape[1]
    group_size = math.gcd(brick_count, 8)
    flat_weight = weight.transpose(1, 0, 2).reshape(out_channels, 27 * channels)

    def per_group(inputs):
        vox_group, ghost_group = inputs
        patches = tap_inputs(vox_group, ghost_group).reshape(group_size, 27 * channels, 512)
        return jnp.einsum("ok,bkv->bov", flat_weight, patches, preferred_element_type=jnp.float32)

    grouped_vox = vox.reshape(brick_count // group_size, group_size, channels, 512)
    grouped_ghost = ghosts.reshape(brick_count // group_size, group_size, 3, channels, 512)
    summed = lax.map(per_group, (grouped_vox, grouped_ghost))
    return summed.reshape(brick_count, out_channels, 512)


def rms_norm(mixed_in, norm_gain):
    scale_row = lax.rsqrt(jnp.mean(mixed_in * mixed_in, axis=-1, keepdims=True) + 1e-06)
    return (mixed_in * scale_row * norm_gain[None, :]).astype(jnp.bfloat16)


def attend_windows(query_ext, kv_ext, alive_ext):
    feat_count, length = query_ext.shape
    count = length // WIN
    head_count = feat_count // HD
    diagonal = jnp.eye(WIN, dtype=bool)

    def per_window(index, result):
        query_heads = query_ext.reshape(head_count, HD, WIN)
        key_heads = kv_ext[0].reshape(head_count, HD, WIN)
        value_heads = kv_ext[1].reshape(head_count, HD, WIN)
        scores = jnp.einsum(
            "hdq,hdk->hqk", query_heads, key_heads, preferred_element_type=jnp.float32
        ) * HD ** (-0.5)
        allowed = (alive_ext[None, None, :] > 0) | diagonal[None]
        row_peak = jnp.max(jnp.where(allowed, scores, -1e30), axis=-1, keepdims=True)
        raw = jnp.where(allowed, jnp.exp(scores - row_peak), 0.0)
        weights_bf = (raw / jnp.sum(raw, axis=-1, keepdims=True)).astype(jnp.bfloat16)
        output = jnp.einsum(
            "hqk,hdk->hdq", weights_bf, value_heads, preferred_element_type=jnp.float32
        )
        output = output.astype(jnp.bfloat16).reshape(feat_count, WIN)
        return output

    empty = jnp.zeros((feat_count, length), jnp.bfloat16)
    return lax.fori_loop(0, count, per_window, empty)


def local(
    features,
    occupancy,
    neighbours,
    conv_weight,
    conv_bias,
    latent,
    token_proj,
    norm_gain,
    qkv_weight,
    out_weight,
):
    my_index = lax.axis_index(("space", "chan"))
    brick_count, channels = (features.shape[0], features.shape[1])
    alive_bf = occupancy.astype(jnp.bfloat16)
    masked = features * alive_bf[:, None, None]
    has_peer = neighbours >= 0
    peer_index = jnp.where(has_peer, neighbours, 0)
    source = jnp.clip(peer_index // brick_count - my_index, -REACH, REACH)
    face_row = ((source + REACH) * brick_count + peer_index % brick_count) * 6 + jnp.arange(
        6, dtype=jnp.int32
    )[None, :]
    own_faces = jnp.einsum(
        "bcv,vfk->bfck", masked, take_table(), preferred_element_type=jnp.float32
    )
    own_faces = own_faces.astype(jnp.bfloat16).reshape(brick_count, 6, channels * 64)
    received = {0: own_faces}
    for spread in range(-REACH, REACH + 1):
        if spread != 0:
            received[spread] = passed_along(own_faces, ("space", "chan"), -spread)
    face_store = jnp.concatenate([received[spread] for spread in range(-REACH, REACH + 1)], axis=0)
    face_store = face_store.reshape(-1, channels * 64)
    picked = jnp.take(face_store, face_row.reshape(-1), axis=0).reshape(
        brick_count, 6, channels * 64
    )
    gathered = jnp.where(has_peer[:, :, None], picked, jnp.zeros_like(picked))
    sheets = gathered.reshape(brick_count, 3, 2, channels, 64)
    ghosts = jnp.einsum(
        "bgsck,gskv->bgcv", sheets, place_table(), preferred_element_type=jnp.float32
    ).astype(jnp.bfloat16)
    summed = convolve(masked, ghosts, conv_weight)
    alive_f = occupancy.astype(jnp.float32)
    mixed = masked.astype(jnp.float32) + jax.nn.silu(summed + conv_bias[None, :, None])
    conv_out = (alive_f[:, None, None] * mixed).astype(jnp.bfloat16)
    pooled = jnp.einsum(
        "bcv,vm->bcm", conv_out, pool_table(), preferred_element_type=jnp.float32
    ).astype(jnp.bfloat16)
    lifted = jnp.einsum("bcm,cd->bmd", pooled, token_proj, preferred_element_type=jnp.float32)
    mixed_in = latent.astype(jnp.float32) + lifted.reshape(brick_count * 64, token_proj.shape[1])
    normed = rms_norm(mixed_in, norm_gain)
    projected = lax.dot_general(
        qkv_weight, normed, (((1,), (1,)), ((), ())), preferred_element_type=jnp.float32
    ).astype(jnp.bfloat16)
    tok_count = projected.shape[2]
    token_alive = jnp.broadcast_to(occupancy[:, None], (brick_count, 64)).reshape(tok_count)
    half_win = WIN // 2
    prev_proj, prev_alive = shifted(
        (projected[:, :, tok_count - half_win :], token_alive[tok_count - half_win :]),
        ("space", "chan"),
        1,
    )
    proj_ext = jnp.concatenate([prev_proj, projected[:, :, : tok_count - half_win]], axis=2)
    alive_ext = jnp.concatenate([prev_alive, token_alive[: tok_count - half_win]], axis=0)
    computed = attend_windows(proj_ext[0], proj_ext[1:3], alive_ext)
    returned = shifted(computed[:, :half_win], ("space", "chan"), -1)
    attended = jnp.concatenate([computed[:, half_win:], returned], axis=1)
    mixing = lax.dot_general(
        out_weight, attended, (((0,), (0,)), ((), ())), preferred_element_type=jnp.float32
    )
    tokens_out = (mixed_in.T + mixing).astype(jnp.bfloat16)
    return (conv_out, tokens_out)


def solution(mesh):
    return jax.shard_map(
        local,
        mesh=mesh,
        in_specs=(
            P(("space", "chan"), None, None),
            P(("space", "chan")),
            P(("space", "chan"), None),
            P(),
            P(),
            P(("space", "chan"), None),
            P(),
            P(),
            P(),
            P(),
        ),
        out_specs=(P(("space", "chan"), None, None), P(None, ("space", "chan"))),
        check_vma=False,
    )
```

profile of v0, /device:TPU:15, one launch (start us, length us, event | category | flops | bytes accessed | tf_op | source)
XLA Modules:
  0.0 164.8 jit_solution(18247109654558557653)
XLA Ops:
  0.6 0.8 fusion.128
  1.4 1.1 broadcast_multiply_fusion
  2.6 1.6 fusion.64
  4.2 0.6 reshape.611
  5.1 2.1 %collective-permute-start.3 = (bf16[16,6,2048]{2,0,1:T(8,128)(2,1)S(1)}, bf16[16,6,2048]{2,0,1:T(8,128)(2,1)}, u32[]{:S(2)}, u32[]{:S(2)}) collective-permute-start(bf16[16,6,2048]{2,0,1:T(8,128)(2,1)S(1)} %copy.93), channel_id=1, source_target_pairs={{2,0},{3,1},{4,2},{5,3},{6,4},{7,5},{8,6},{9,7},{10,8},{11,9},{12,... | collective-permute-start | bytes 1179656 | tf_op jit(solution)/shard_map/ppermute | solution.py:17
  7.2 2.9 %collective-permute-start.2 = (bf16[16,6,2048]{2,0,1:T(8,128)(2,1)S(1)}, bf16[16,6,2048]{2,0,1:T(8,128)(2,1)}, u32[]{:S(2)}, u32[]{:S(2)}) collective-permute-start(bf16[16,6,2048]{2,0,1:T(8,128)(2,1)S(1)} %copy.93), channel_id=1, source_target_pairs={{1,0},{2,1},{3,2},{4,3},{5,4},{6,5},{7,6},{8,7},{9,8},{10,9},{11,1... | collective-permute-start | bytes 1179656 | tf_op jit(solution)/shard_map/ppermute | solution.py:17
  10.1 4.8 %collective-permute-start.1 = (bf16[16,6,2048]{2,0,1:T(8,128)(2,1)S(1)}, bf16[16,6,2048]{2,0,1:T(8,128)(2,1)}, u32[]{:S(2)}, u32[]{:S(2)}) collective-permute-start(bf16[16,6,2048]{2,0,1:T(8,128)(2,1)S(1)} %copy.93), channel_id=1, source_target_pairs={{0,1},{1,2},{2,3},{3,4},{4,5},{5,6},{6,7},{7,8},{8,9},{9,10},{10,1... | collective-permute-start | bytes 1179656 | tf_op jit(solution)/shard_map/ppermute | solution.py:17
  14.9 2.8 %collective-permute-start = (bf16[16,6,2048]{2,0,1:T(8,128)(2,1)S(1)}, bf16[16,6,2048]{2,0,1:T(8,128)(2,1)}, u32[]{:S(2)}, u32[]{:S(2)}) collective-permute-start(bf16[16,6,2048]{2,0,1:T(8,128)(2,1)S(1)} %copy.93), channel_id=1, source_target_pairs={{0,2},{1,3},{2,4},{3,5},{4,6},{5,7},{6,8},{7,9},{8,10},{9,11},{10,... | collective-permute-start | bytes 1179656 | tf_op jit(solution)/shard_map/ppermute | solution.py:17
  17.7 0.7 broadcast_compare_fusion
  18.4 0.7 fusion.89
  19.6 1.0 copy.82
  20.9 15.6 %collective-permute-done = bf16[16,6,2048]{2,0,1:T(8,128)(2,1)} collective-permute-done((bf16[16,6,2048]{2,0,1:T(8,128)(2,1)S(1)}, bf16[16,6,2048]{2,0,1:T(8,128)(2,1)}, u32[]{:S(2)}, u32[]{:S(2)}) %collective-permute-start) | collective-permute-done | bytes 393248 | tf_op jit(solution)/shard_map/ppermute | solution.py:17
  36.5 1.0 constant_dynamic-update-slice_fusion.4
  37.6 1.0 constant_dynamic-update-slice_fusion.3
  38.8 1.0 constant_dynamic-update-slice_fusion.1
  39.9 1.0 constant_dynamic-update-slice_fusion
  40.9 2.6 %copy.79 = bf16[80,6,2048]{2,1,0:T(8,128)(2,1)} copy(bf16[80,6,2048]{2,0,1:T(8,128)(2,1)S(1)} %constant_dynamic-update-slice_fusion) | data formatting | bytes 3932160 | tf_op jit(solution)/shard_map/concatenate | solution.py:200
  43.5 4.1 %reshape.588 = bf16[480,2048]{1,0:T(8,128)(2,1)} reshape(bf16[80,6,2048]{2,1,0:T(8,128)(2,1)} %copy.79) | data formatting | bytes 3932160 | tf_op jit(solution)/shard_map/reshape | solution.py:201
  47.6 3.0 %gather_fusion = bf16[96,2048]{1,0:T(8,128)(2,1)S(1)} fusion(bf16[480,2048]{1,0:T(8,128)(2,1)} %reshape.588, s32[1024]{0:T(1024)S(1)} %pad_clamp_fusion), kind=kCustom, calls=%fused_computation | custom fusion | bytes 786816 | tf_op jit(solution)/shard_map/jit(_take)/gather | solution.py:202
  50.6 0.8 gather.7
  51.4 3.2 %bitcast_convert_fusion = bf16[3,16,32,512]{3,2,1,0:T(8,128)(2,1)} fusion(bf16[3,2,64,512,1]{3,2,1,4,0:T(8,128)(2,1)} %constant.650, bf16[16,3,2,32,64]{4,3,2,1,0:T(8,128)(2,1)S(1)} %gather.7, pred[16,3,2]{2,0,1:T(8,128)(4,1)S(1)} %copy.77, pred[16,3,2]{2,0,1:T(8,128)(4,1)S(1)} %copy.76), kind=kOutput, calls=%fused_computation.200 | convolution fusion | flops 202506240 | bytes 2359488 | tf_op jit(solution)/shard_map/bgsck,gskv->bgcv/dot_general | solution.py:207
  54.6 29.6 %while.17 = (s32[]{:T(128)}, f32[2,8,32,512]{3,2,1,0:T(8,128)}, bf16[2,8,32,512]{3,2,1,0:T(8,128)(2,1)S(1)}, bf16[2,8,3,32,512]{4,3,1,0,2:T(8,128)(2,1)}, bf16[32,864]{1,0:T(8,128)(2,1)S(1)}, /*index=5*/s32[]{:T(128)}) while((s32[]{:T(128)}, f32[2,8,32,512]{3,2,1,0:T(8,128)}, bf16[2,8,32,512]{3,2,1,0:T(8,128)(2,1)S(1)}, ...), condition=%wide.region_1.2_spmd, body=%wide.region_0.1_spmd.sunk | while | flops 270078464 | bytes 78502576 | solution.py:134
  58.6 0.3 fusion.176
  59.5 0.5 bitcast_dynamic-update-slice_fusion.52
  60.0 0.5 bitcast_dynamic-update-slice_fusion.53
  60.5 0.6 bitcast_dynamic-update-slice_fusion.54
  61.1 0.5 bitcast_dynamic-update-slice_fusion.55
  61.8 0.3 bitcast_dynamic-update-slice_fusion.57
  62.1 0.5 bitcast_dynamic-update-slice_fusion.58
  62.6 0.3 bitcast_dynamic-update-slice_fusion.59
  62.9 0.5 bitcast_dynamic-update-slice_fusion.60
  63.4 0.5 bitcast_dynamic-update-slice_fusion.61
  64.1 0.3 bitcast_dynamic-update-slice_fusion.63
  67.3 1.3 fusion.193
  68.6 1.0 copy-done.8
  74.3 0.5 bitcast_dynamic-update-slice_fusion.52
  74.7 0.5 bitcast_dynamic-update-slice_fusion.53
  75.2 0.6 bitcast_dynamic-update-slice_fusion.54
  75.8 0.5 bitcast_dynamic-update-slice_fusion.55
  76.5 0.3 bitcast_dynamic-update-slice_fusion.57
  76.8 0.5 bitcast_dynamic-update-slice_fusion.58
  77.3 0.3 bitcast_dynamic-update-slice_fusion.59
  77.7 0.5 bitcast_dynamic-update-slice_fusion.60
  78.1 0.5 bitcast_dynamic-update-slice_fusion.61
  78.8 0.3 bitcast_dynamic-update-slice_fusion.63
  82.0 1.3 fusion.193
  83.3 1.0 copy-done.8
  84.3 1.7 %multiply_convert_fusion.1 = bf16[16,32,512]{2,1,0:T(8,128)(2,1)S(1)} fusion(f32[2,8,32,512]{3,2,1,0:T(8,128)} %get-tuple-element.112, f32[32]{0:T(128)S(1)} %copy-done.14, f32[16]{0:T(128)S(1)} %get-tuple-element.275, bf16[16,32,512]{2,1,0:T(8,128)(2,1)S(1)} %copy-done.5, bf16[16]{0:T(256)(128)(2,1)S(1)} %get-tuple-element.276), kind=kLoop, calls=%fused_computation.222 | loop fusion | flops 2621440 | bytes 2097376 | tf_op jit(solution)/shard_map/convert_element_type | solution.py:213
  86.0 2.3 %fusion.65 = f32[16,64,512]{2,1,0:T(8,128)} fusion(bf16[16,32,512]{2,1,0:T(8,128)(2,1)S(1)} %multiply_convert_fusion.1, bf16[512,64,1]{1,0,2:T(8,128)(2,1)S(1)} %copy-done.11, bf16[32,512]{1,0:T(8,128)(2,1)S(1)} %copy-done.12), kind=kOutput, calls=%fused_computation.211 | convolution fusion | flops 67141632 | bytes 2719744 | tf_op jit(solution)/shard_map/bcm,cd->bmd/dot_general | solution.py:217
  88.2 2.2 %multiply_reduce_fusion = (f32[1024]{0:T(1024)S(1)}, f32[1024,512]{1,0:T(8,128)S(1)}) fusion(f32[16,64,512]{2,1,0:T(8,128)} %fusion.65, bf16[1024,512]{1,0:T(8,128)(2,1)} %param.20), kind=kLoop, calls=%fused_computation.205 | loop fusion | flops 2096128 | bytes 5246976 | tf_op jit(solution)/shard_map/reduce_sum | solution.py:139
  90.5 1.9 %convert_bitcast_fusion = bf16[3,512,1024]{1,2,0:T(8,128)(2,1)S(1)} fusion(bf16[3,512,512]{2,1,0:T(8,128)(2,1)S(1)} %copy-done, f32[1024,512]{1,0:T(8,128)S(1)} %get-tuple-element.270, f32[512]{0:T(512)S(1)} %copy-done.15, f32[1024]{0:T(1024)S(1)} %add_rsqrt_fusion), kind=kOutput, calls=%fused_computation.201 | convolution fusion | flops 1613758464 | bytes 6821888 | tf_op jit(solution)/shard_map/dot_general | solution.py:220
  92.4 1.4 fusion.125
  94.1 17.3 %collective-permute-done.5 = s32[512]{0:T(512)S(1)} collective-permute-done((s32[512]{0:T(512)S(1)}, s32[512]{0:T(512)S(1)}, u32[]{:S(2)}, u32[]{:S(2)}) %collective-permute-start.5) | collective-permute-done | bytes 2080 | tf_op jit(solution)/shard_map/ppermute | solution.py:22
  111.4 1.4 fusion.59
  112.8 2.9 %pad_maximum_fusion = (bf16[1,512,1024]{1,2,0:T(8,128)(2,1)}, bf16[1,512,1024]{1,2,0:T(8,128)(2,1)}, bf16[1,512,1024]{1,2,0:T(8,128)(2,1)S(1)}) fusion(bf16[3,512,512]{1,2,0:T(8,128)(2,1)S(1)} %get-tuple-element.267, bf16[3,512,512]{1,2,0:T(8,128)(2,1)} %collective-permute-done.4), kind=kLoop, calls=%fused_computation.215 | loop fusion | flops 6291456 | bytes 6291456 | tf_op jit(solution)/shard_map/concatenate | solution.py:231
  115.7 1.5 copy.86
  117.2 2.3 %copy.84 = bf16[1,512,1024]{2,1,0:T(8,128)(2,1)} copy(bf16[1,512,1024]{1,2,0:T(8,128)(2,1)} %get-tuple-element.265) | data formatting | bytes 2097152 | tf_op jit(solution)/shard_map/while/body/eval_jaxpr/slice | solution.py:152
  119.4 0.5 copy.85
  120.0 19.0 %fusion.129 = (f32[8,1024]{1,0:T(8,128)S(1)}, f32[8,1024,1024]{1,2,0:T(8,128)}) fusion(pred[1024,1024]{0,1:T(8,128)(4,1)} %fusion.59, bf16[8,64,1024]{2,1,0:T(8,128)(2,1)S(1)} %bitcast.287, bf16[8,64,1024]{2,1,0:T(8,128)(2,1)S(1)} %bitcast.286), kind=kOutput, calls=%fused_computation.296 | convolution fusion | flops 2197816320 | bytes 36732928 | tf_op jit(solution)/shard_map/while/body/eval_jaxpr/sub | solution.py:158
  139.0 12.5 %fusion.62 = bf16[8,64,1024]{2,1,0:T(8,128)(2,1)S(1)} fusion(bf16[8,64,1024]{2,1,0:T(8,128)(2,1)S(1)} %bitcast.285, f32[8,1024,1024]{1,2,0:T(8,128)} %get-tuple-element.278, f32[8,1024]{1,0:T(8,128)S(1)} %get-tuple-element.277), kind=kOutput, calls=%fused_computation.206 | convolution fusion | flops 1091043328 | bytes 35684352 | tf_op jit(solution)/shard_map/while/body/eval_jaxpr/hqk,hdk->hdq/dot_general | solution.py:160
  151.6 0.6 collective-permute-start.6
  152.2 10.6 %collective-permute-done.6 = bf16[512,512]{1,0:T(8,128)(2,1)S(1)} collective-permute-done((bf16[512,512]{1,0:T(8,128)(2,1)S(1)}, bf16[512,512]{1,0:T(8,128)(2,1)S(1)}, u32[]{:S(2)}, u32[]{:S(2)}) %collective-permute-start.6) | collective-permute-done | bytes 524320 | tf_op jit(solution)/shard_map/ppermute | solution.py:22
  162.8 0.8 fusion.63
  163.5 1.3 copy.88
  (240 shorter events, 16.2 us)
Async XLA Ops:
  0.6 89.8 %copy-start = (bf16[3,512,512]{2,1,0:T(8,128)(2,1)S(1)}, bf16[3,512,512]{2,1,0:T(8,128)(2,1)}, u32[]{:S(2)}) copy-start(bf16[3,512,512]{2,1,0:T(8,128)(2,1)} %param.23) | copy-start | bytes 4718596
  5.1 34.8 %collective-permute-start.3 = (bf16[16,6,2048]{2,0,1:T(8,128)(2,1)S(1)}, bf16[16,6,2048]{2,0,1:T(8,128)(2,1)}, u32[]{:S(2)}, u32[]{:S(2)}) collective-permute-start(bf16[16,6,2048]{2,0,1:T(8,128)(2,1)S(1)} %copy.93), channel_id=1, source_target_pairs={{2,0},{3,1},{4,2},{5,3},{6,4},{7,5},{8,6},{9,7},{10,8},{11,9},{12,... | collective-permute-start | bytes 1179656 | tf_op jit(solution)/shard_map/ppermute | solution.py:17
  7.2 31.6 %collective-permute-start.2 = (bf16[16,6,2048]{2,0,1:T(8,128)(2,1)S(1)}, bf16[16,6,2048]{2,0,1:T(8,128)(2,1)}, u32[]{:S(2)}, u32[]{:S(2)}) collective-permute-start(bf16[16,6,2048]{2,0,1:T(8,128)(2,1)S(1)} %copy.93), channel_id=1, source_target_pairs={{1,0},{2,1},{3,2},{4,3},{5,4},{6,5},{7,6},{8,7},{9,8},{10,9},{11,1... | collective-permute-start | bytes 1179656 | tf_op jit(solution)/shard_map/ppermute | solution.py:17
  10.1 27.5 %collective-permute-start.1 = (bf16[16,6,2048]{2,0,1:T(8,128)(2,1)S(1)}, bf16[16,6,2048]{2,0,1:T(8,128)(2,1)}, u32[]{:S(2)}, u32[]{:S(2)}) collective-permute-start(bf16[16,6,2048]{2,0,1:T(8,128)(2,1)S(1)} %copy.93), channel_id=1, source_target_pairs={{0,1},{1,2},{2,3},{3,4},{4,5},{5,6},{6,7},{7,8},{8,9},{9,10},{10,1... | collective-permute-start | bytes 1179656 | tf_op jit(solution)/shard_map/ppermute | solution.py:17
  14.9 21.6 %collective-permute-start = (bf16[16,6,2048]{2,0,1:T(8,128)(2,1)S(1)}, bf16[16,6,2048]{2,0,1:T(8,128)(2,1)}, u32[]{:S(2)}, u32[]{:S(2)}) collective-permute-start(bf16[16,6,2048]{2,0,1:T(8,128)(2,1)S(1)} %copy.93), channel_id=1, source_target_pairs={{0,2},{1,3},{2,4},{3,5},{4,6},{5,7},{6,8},{7,9},{8,10},{9,11},{10,... | collective-permute-start | bytes 1179656 | tf_op jit(solution)/shard_map/ppermute | solution.py:17
  54.6 29.6 %copy-start.5 = (bf16[16,32,512]{2,1,0:T(8,128)(2,1)S(1)}, bf16[16,32,512]{2,1,0:T(8,128)(2,1)}, u32[]{:S(2)}) copy-start(bf16[16,32,512]{2,1,0:T(8,128)(2,1)} %param.15) | copy-start | bytes 1572868
  54.6 29.6 %copy-start.14 = (f32[32]{0:T(128)S(1)}, f32[32]{0:T(128)}, u32[]{:S(2)}) copy-start(f32[32]{0:T(128)} %param.19) | copy-start | bytes 388
  54.6 31.3 %copy-start.11 = (bf16[512,64,1]{1,0,2:T(8,128)(2,1)S(1)}, bf16[512,64,1]{1,0,2:T(8,128)(2,1)}, u32[]{:S(2)}) copy-start(bf16[512,64,1]{1,0,2:T(8,128)(2,1)} %constant.651) | copy-start | bytes 196612
  54.6 31.3 %copy-start.12 = (bf16[32,512]{1,0:T(8,128)(2,1)S(1)}, bf16[32,512]{1,0:T(8,128)(2,1)}, u32[]{:S(2)}) copy-start(bf16[32,512]{1,0:T(8,128)(2,1)} %param.21) | copy-start | bytes 98308
  55.6 1.9 %copy-start.2 = (bf16[2,8,3,32,512]{4,3,1,0,2:T(8,128)(2,1)S(1)}, bf16[2,8,3,32,512]{4,3,1,0,2:T(8,128)(2,1)}, u32[]{:S(2)}) copy-start(bf16[2,8,3,32,512]{4,3,1,0,2:T(8,128)(2,1)} %get-tuple-element.567) | copy-start | bytes 4718596 | tf_op jit(solution)/shard_map/while
  64.7 2.6 %copy-start.7 = (f32[2,8,32,512]{3,2,1,0:T(8,128)S(1)}, f32[2,8,32,512]{3,2,1,0:T(8,128)}, u32[]{:S(2)}) copy-start(f32[2,8,32,512]{3,2,1,0:T(8,128)} %get-tuple-element.559) | copy-start | bytes 3145732 | tf_op jit(solution)/shard_map/while
  68.6 1.0 copy-start.8
  70.3 1.9 %copy-start.2 = (bf16[2,8,3,32,512]{4,3,1,0,2:T(8,128)(2,1)S(1)}, bf16[2,8,3,32,512]{4,3,1,0,2:T(8,128)(2,1)}, u32[]{:S(2)}) copy-start(bf16[2,8,3,32,512]{4,3,1,0,2:T(8,128)(2,1)} %get-tuple-element.567) | copy-start | bytes 4718596 | tf_op jit(solution)/shard_map/while
  79.4 2.6 %copy-start.7 = (f32[2,8,32,512]{3,2,1,0:T(8,128)S(1)}, f32[2,8,32,512]{3,2,1,0:T(8,128)}, u32[]{:S(2)}) copy-start(f32[2,8,32,512]{3,2,1,0:T(8,128)} %get-tuple-element.559) | copy-start | bytes 3145732 | tf_op jit(solution)/shard_map/while
  83.3 1.0 copy-start.8
  84.3 6.2 %copy-start.15 = (f32[512]{0:T(512)S(1)}, f32[512]{0:T(512)}, u32[]{:S(2)}) copy-start(f32[512]{0:T(512)} %param.22) | copy-start | bytes 6148
  86.0 6.4 %copy-start.6 = (bf16[16,32,512]{2,1,0:T(8,128)(2,1)}, bf16[16,32,512]{2,1,0:T(8,128)(2,1)S(1)}, u32[]{:S(2)}) copy-start(bf16[16,32,512]{2,1,0:T(8,128)(2,1)S(1)} %multiply_convert_fusion.1) | copy-start | bytes 1572868
  90.4 3.3 %copy-start.3 = (f32[1024,512]{1,0:T(8,128)}, f32[1024,512]{1,0:T(8,128)S(1)}, u32[]{:S(2)}) copy-start(f32[1024,512]{1,0:T(8,128)S(1)} %get-tuple-element.270) | copy-start | bytes 6291460
  90.5 3.3 %copy-start.13 = (s32[16]{0:T(128)S(1)}, s32[16]{0:T(128)}, u32[]{:S(2)}) copy-start(s32[16]{0:T(128)} %param.16) | copy-start | bytes 196
  93.7 19.1 %collective-permute-start.4 = (bf16[3,512,512]{1,2,0:T(8,128)(2,1)}, bf16[3,512,512]{1,2,0:T(8,128)(2,1)}, u32[]{:S(2)}, u32[]{:S(2)}) collective-permute-start(bf16[3,512,512]{1,2,0:T(8,128)(2,1)} %get-tuple-element.268), channel_id=1, source_target_pairs={{0,1},{1,2},{2,3},{3,4},{4,5},{5,6},{6,7},{7,8},{8,9},{9,10},{10,1... | collective-permute-start | bytes 4718600 | tf_op jit(solution)/shard_map/ppermute | solution.py:22
  94.0 17.4 %collective-permute-start.5 = (s32[512]{0:T(512)S(1)}, s32[512]{0:T(512)S(1)}, u32[]{:S(2)}, u32[]{:S(2)}) collective-permute-start(s32[512]{0:T(512)S(1)} %slice.488), channel_id=1, source_target_pairs={{0,1},{1,2},{2,3},{3,4},{4,5},{5,6},{6,7},{7,8},{8,9},{9,10},{10,1... | collective-permute-start | bytes 6152 | tf_op jit(solution)/shard_map/ppermute | solution.py:22
  120.0 19.0 %copy-start.9 = (bf16[1,512,1024]{2,1,0:T(8,128)(2,1)S(1)}, bf16[1,512,1024]{2,1,0:T(8,128)(2,1)}, u32[]{:S(2)}) copy-start(bf16[1,512,1024]{2,1,0:T(8,128)(2,1)} %copy.84) | copy-start | bytes 3145732
  139.0 23.8 %copy-start.4 = (f32[1024,512]{1,0:T(8,128)S(1)}, f32[1024,512]{1,0:T(8,128)}, u32[]{:S(2)}) copy-start(f32[1024,512]{1,0:T(8,128)} %copy-done.3) | copy-start | bytes 6291460
  139.0 23.8 %copy-start.10 = (bf16[512,512]{1,0:T(8,128)(2,1)S(1)}, bf16[512,512]{1,0:T(8,128)(2,1)}, u32[]{:S(2)}) copy-start(bf16[512,512]{1,0:T(8,128)(2,1)} %param.24) | copy-start | bytes 1572868
  139.0 25.8 %copy-start.1 = (bf16[3,512,512]{2,1,0:T(8,128)(2,1)S(1)}, bf16[3,512,512]{2,1,0:T(8,128)(2,1)}, u32[]{:S(2)}) copy-start(bf16[3,512,512]{2,1,0:T(8,128)(2,1)} %param.23) | copy-start | bytes 4718596
  151.6 11.2 %collective-permute-start.6 = (bf16[512,512]{1,0:T(8,128)(2,1)S(1)}, bf16[512,512]{1,0:T(8,128)(2,1)S(1)}, u32[]{:S(2)}, u32[]{:S(2)}) collective-permute-start(bf16[512,512]{1,0:T(8,128)(2,1)S(1)} %get-tuple-element.272), channel_id=1, source_target_pairs={{0,31},{1,0},{2,1},{3,2},{4,3},{5,4},{6,5},{7,6},{8,7},{9,8},{10,9... | collective-permute-start | bytes 1572872 | tf_op jit(solution)/shard_map/ppermute | solution.py:22
where the time goes:
time: 166 us; the launch traced here: 165 us
  matrix products  43.7 us (26%)
  waiting for transfers between devices  43.5 us (26%)
  local copies, waits for them, and re-layouts  34.4 us (21%)
  other arithmetic  27.8 us (17%)
  starting transfers between devices  13.3 us (8%)
    ppermute x3, waiting for transfers between devices, shifted(): lax.ppermute(array, axis, [(i, (i + by) % size) for i in range(size)])  27.9 us
    sub x1, matrix products, per_window(): raw = jnp.where(allowed, jnp.exp(scores - row_peak), 0.0)  19 us
    ppermute x4, waiting for transfers between devices, passed_along(): lax.ppermute(value, axis, [(source, source + steps) for source in range(f...  15.7 us
    while x52, other arithmetic  14.7 us
    ppermute x4, starting transfers between devices, passed_along(): lax.ppermute(value, axis, [(source, source + steps) for source in range(f...  12.6 us
    dot_general x1, matrix products, per_window(): jnp.einsum('hqk,hdk->hdq', weights_bf, value_heads, preferred_element_typ...  12.5 us
    slice x44, local copies, waits for them, and re-layouts, shift_lanes(): return jnp.concatenate([source[..., offset:], filler], axis=-1)  7.19 us
    unnamed x31, local copies, waits for them, and re-layouts  4.67 us
  transfers between devices with their start and end apart: 7, of which 3 were waited for; matrix products, arithmetic and copies ran while one was open for 5% of the time, Pallas kernels for 0%

commit v1 on v0

v1 whole, which is shorter than its diff:
```python
import math

import jax
import jax.numpy as jnp
import numpy as np
from jax import lax
from jax.experimental import pallas as pl
from jax.experimental.pallas import tpu as pltpu
from jax.sharding import PartitionSpec as P

HD = 64
WIN = 1024
REACH = 2
AXES = ("space", "chan")
NEG = -1e30
TILES = 96
F32 = jnp.float32
BF16 = jnp.bfloat16
VM = pltpu.VMEM
ANY = pl.ANY


def vmem(count):
    return [pl.BlockSpec(memory_space=pltpu.VMEM)] * count


def smem(count):
    return [pl.BlockSpec(memory_space=pltpu.SMEM)] * count


def anyspace(count):
    return [pl.BlockSpec(memory_space=pl.ANY)] * count


def cost(flops, moved, trans=0):
    return pl.CostEstimate(flops=flops, bytes_accessed=moved, transcendentals=trans)


def swap_blocks(four):
    lane = lax.broadcasted_iota(jnp.int32, four[0].shape, 1)
    low = lane < 64
    even = (lane // 32) % 2 == 0
    half = []
    for a, b in ((0, 2), (1, 3)):
        half.append(jnp.where(low, four[a], pltpu.roll(four[b], 64, 1)))
        half.append(jnp.where(low, pltpu.roll(four[a], 64, 1), four[b]))
    a0, a2, a1, a3 = half
    return [
        jnp.where(even, a0, pltpu.roll(a1, 32, 1)),
        jnp.where(even, pltpu.roll(a0, 96, 1), a1),
        jnp.where(even, a2, pltpu.roll(a3, 32, 1)),
        jnp.where(even, pltpu.roll(a2, 96, 1), a3),
    ]


def prep_kernel(occ, feat, xb, faces, turned, wide):
    for g in range(4):
        rows = [
            feat[4 * g + j].astype(F32) * (occ[4 * g + j]).astype(F32) for j in range(4)
        ]
        turned[g] = jnp.concatenate(rows, axis=0).T
    for g in range(4):
        sheets = [turned[g, pl.ds(z, 64, stride=8), :] for z in range(8)]
        for face, z in ((0, 0), (1, 7)):
            for xq in range(4):
                tile = jnp.concatenate(
                    [sheets[z][8 * xq : 8 * xq + 8], sheets[z][8 * xq + 32 : 8 * xq + 40]], axis=1
                )
                faces[64 + (2 * g + face) * 4 + xq] = tile.astype(BF16)
        for half in range(2):
            for j, block in enumerate(swap_blocks(sheets[4 * half : 4 * half + 4])):
                wide[half, 4 * g + j] = block
                xb[4 * g + j, :, 128 * half : 128 * half + 128] = block
    for b in range(16):
        for half in range(2):
            lanes = slice(128 * half, 128 * half + 128)
            faces[4 * b, :, lanes] = wide[half, b, 56:64, :].astype(BF16)
            faces[4 * b + 1, :, lanes] = wide[half, b, 0:8, :].astype(BF16)
            faces[4 * b + 2, :, lanes] = wide[half, b, pl.ds(7, 8, stride=8), :].astype(BF16)
            faces[4 * b + 3, :, lanes] = wide[half, b, pl.ds(0, 8, stride=8), :].astype(BF16)


def prep(occ, feat):
    return pl.pallas_call(
        prep_kernel,
        name="prep",
        out_shape=(
            jax.ShapeDtypeStruct((16, 64, 256), F32),
            jax.ShapeDtypeStruct((TILES, 8, 256), BF16),
        ),
        in_specs=smem(1) + vmem(1),
        out_specs=tuple(vmem(2)),
        scratch_shapes=[VM((4, 512, 128), F32), VM((2, 16, 64, 128), F32)],
        cost_estimate=cost(1 << 20, 2 << 20),
    )(occ, feat)


def shifted_rows(tile, step):
    if step == 0:
        return tile
    row = lax.broadcasted_iota(jnp.int32, tile.shape, 0) % 8
    if step < 0:
        moved = pltpu.roll(tile, 1, 0)
        return jnp.where(row == 0, 0.0, moved)
    moved = pltpu.roll(tile, tile.shape[0] - 1, 0)
    return jnp.where(row == 7, 0.0, moved)


def write_patches(lhs, brick, tiles):
    zero = jnp.zeros((8, 256), F32)
    rows = pl.ds(pl.multiple_of(brick * 64, 64), 64)
    for dy in (-1, 0, 1):
        moved = [shifted_rows(t, dy) for t in tiles]
        for dx in (-1, 0, 1):
            picked = [moved[x + dx] if 0 <= x + dx < 8 else zero for x in range(8)]
            tap = (dx + 1) * 3 + dy + 1
            lhs[rows, 256 * tap : 256 * tap + 256] = jnp.concatenate(picked, axis=0).astype(BF16)


def bands_kernel(taps, spread, band, band_z, wide):
    wide[...] = jnp.dot(taps[...], spread[...], preferred_element_type=F32)
    block = lax.broadcasted_iota(jnp.int32, (32, 256), 1) // 32

    def per_tap(t, carry):
        base = [
            wide[pl.ds(pl.multiple_of((t * 3 + k) * 32, 32), 32), :] for k in range(3)
        ]
        for z in range(8):
            value = jnp.where(block == z, base[1], 0.0)
            value = jnp.where(block == z + 1, base[0], value)
            value = jnp.where(block == z - 1, base[2], value)
            band[pl.ds(pl.multiple_of(t * 256 + 32 * z, 32), 32), :] = value.astype(BF16)
        for face, k in ((0, 0), (1, 2)):
            value = jnp.where(block == 7 * face, base[k], 0.0).astype(BF16)
            for j in range(4):
                start = pl.multiple_of(t * 256 + 128 * face + 32 * j, 32)
                band_z[pl.ds(start, 32), :] = value
        return carry

    lax.fori_loop(0, 9, per_tap, 0)


def bands(conv_weight):
    taps = conv_weight.transpose(0, 2, 1).reshape(27 * 32, 32)
    spread = jnp.asarray(np.tile(np.eye(32, dtype=np.float32), (1, 8)), BF16)
    return pl.pallas_call(
        bands_kernel,
        name="bands",
        out_shape=(
            jax.ShapeDtypeStruct((2304, 256), BF16),
            jax.ShapeDtypeStruct((2304, 256), BF16),
        ),
        in_specs=vmem(2),
        out_specs=tuple(vmem(2)),
        scratch_shapes=[VM((864, 256), F32)],
        cost_estimate=cost(1 << 24, 3 << 20),
    )(taps, spread)


def inner_kernel(xb, band, acc, lhs):
    def per_brick(b, carry):
        write_patches(lhs, b, [xb[b, 8 * x : 8 * x + 8, :] for x in range(8)])
        return carry

    lax.fori_loop(0, 16, per_brick, 0)

    def per_rows(i, carry):
        rows = pl.ds(pl.multiple_of(i * 512, 512), 512)
        acc[rows, :] = jnp.dot(lhs[rows, :], band[...], preferred_element_type=F32)
        return carry

    lax.fori_loop(0, 2, per_rows, 0)


def inner(xb, band):
    return pl.pallas_call(
        inner_kernel,
        name="inner",
        out_shape=jax.ShapeDtypeStruct((1024, 256), F32),
        in_specs=vmem(2),
        out_specs=vmem(1)[0],
        scratch_shapes=[VM((1024, 2304), BF16)],
        cost_estimate=cost(2 * 1024 * 2304 * 256, 4 << 20),
    )(xb, band)


def outer_kernel(
    index, occ, core, own, back, ahead, partner, relay, xb, acc, band, band_z, bias, pool, pick,
    latent, proj, gain,
    blocks, pooled, to_partner, to_cross,
    store, lhs, flat, edges, sums, halves, sems,
):
    copies = [
        pltpu.make_async_copy(ref, store.at[slot], sems.at[slot])
        for slot, ref in enumerate((own, back, ahead, partner, relay))
    ]
    for copy in copies:
        copy.start()
    for copy in copies:
        copy.wait()
    lane = lax.broadcasted_iota(jnp.int32, (8, 256), 1) % 128 // 32

    def gather(b, carry):
        for face in range(4):
            at = index[b * 6 + face]
            valid = (at >= 0).astype(F32)
            at = jnp.maximum(at, 0)
            tile = store[at // 16, (at % 16) * 4 + face].astype(F32) * valid
            flat[face, pl.ds(pl.multiple_of(b * 8, 8), 8), :] = tile
        low, high = [], []
        for face, into in ((0, low), (1, high)):
            at = index[b * 6 + 4 + face]
            valid = (at >= 0).astype(F32)
            at = jnp.maximum(at, 0)
            brick = at % 16
            base = 64 + (brick // 4 * 2 + (1 - face)) * 4
            mask = jnp.where(lane == brick % 4, valid, 0.0)
            for xq in range(4):
                into.append(store[at // 16, base + xq].astype(F32) * mask)
        tiles = []
        for x in range(8):
            lanes = slice(128 * (x // 4), 128 * (x // 4) + 128)
            tiles.append(jnp.concatenate([low[x % 4][:, lanes], high[x % 4][:, lanes]], axis=1))
        write_patches(lhs, b, tiles)
        return carry

    lax.fori_loop(0, 16, gather, 0)
    for face in range(4):
        sheet = flat[face]
        side = 0 if face % 2 == 0 else 2
        total = None
        for step in (-1, 0, 1):
            tap = side * 3 + step + 1 if face < 2 else (step + 1) * 3 + side
            part = jnp.dot(
                shifted_rows(sheet, step).astype(BF16),
                band[256 * tap : 256 * tap + 256, :],
                preferred_element_type=F32,
            )
            total = part if total is None else total + part
        edges[face] = total

    def per_rows(i, carry):
        rows = pl.ds(pl.multiple_of(i * 512, 512), 512)
        sums[rows, :] = acc[rows, :] + jnp.dot(
            lhs[rows, :], band_z[...], preferred_element_type=F32
        )
        return carry

    lax.fori_loop(0, 2, per_rows, 0)
    row = lax.broadcasted_iota(jnp.int32, (8, 256), 0)

    def finish(b, carry):
        start = pl.multiple_of(b * 64, 64)
        alive = occ[b].astype(F32)
        sheet_rows = pl.ds(pl.multiple_of(b * 8, 8), 8)
        y_low, y_high = edges[2, sheet_rows, :], edges[3, sheet_rows, :]
        done = []
        for x in range(8):
            total = sums[pl.ds(start + 8 * x, 8), :]
            total = total + jnp.where(row == 0, y_low[x : x + 1, :], 0.0)
            total = total + jnp.where(row == 7, y_high[x : x + 1, :], 0.0)
            if x == 0:
                total = total + edges[0, sheet_rows, :]
            if x == 7:
                total = total + edges[1, sheet_rows, :]
            value = total + bias[...]
            mixed = xb[b, 8 * x : 8 * x + 8, :] + value / (1.0 + jnp.exp(-value))
            done.append(alive * mixed)
        block = jnp.concatenate(done, axis=0).astype(BF16)
        blocks[b] = block.astype(F32)
        cells = jnp.dot(pool[...], block, preferred_element_type=F32) * pick[...]
        cells = cells[:, :128] + cells[:, 128:]
        cells = cells + pltpu.roll(cells, 64, 1)
        cells = cells + pltpu.roll(cells, 32, 1)
        pooled[pl.ds(start, 64), :] = cells.astype(BF16)
        return carry

    lax.fori_loop(0, 16, finish, 0)

    def norm(i, carry):
        rows = pl.ds(pl.multiple_of(i * 256, 256), 256)
        lifted = jnp.dot(pooled[rows, :], proj[...], preferred_element_type=F32)
        mixed = latent[rows, :].astype(F32) + lifted
        scale = lax.rsqrt(jnp.mean(mixed * mixed, axis=-1, keepdims=True) + 1e-06)
        halves[i // 2, pl.ds(pl.multiple_of(i % 2 * 256, 256), 256), :] = (
            mixed * scale * gain[...]
        ).astype(BF16)
        return carry

    lax.fori_loop(0, 4, norm, 0)
    for half in range(2):
        block_row = lax.broadcasted_iota(jnp.int32, (16, 512), 0)
        flags = jnp.zeros((16, 512), F32)
        for b in range(8):
            flags = jnp.where(block_row == b, occ[8 * half + b].astype(F32), flags)
        halves[half, 512:528, :] = flags.astype(BF16)
    out = [
        pltpu.make_async_copy(halves.at[1 - core[0]], to_partner, sems.at[5]),
        pltpu.make_async_copy(halves.at[core[0]], to_cross, sems.at[6]),
    ]
    for copy in out:
        copy.start()
    for copy in out:
        copy.wait()


def outer(index, occ, core, stores, xb, acc, band, band_z, bias, pool, pick, latent, proj, gain):
    return pl.pallas_call(
        outer_kernel,
        name="outer",
        out_shape=(
            jax.ShapeDtypeStruct((16, 64, 256), F32),
            jax.ShapeDtypeStruct((1024, 128), BF16),
            jax.ShapeDtypeStruct((528, 512), BF16),
            jax.ShapeDtypeStruct((528, 512), BF16),
        ),
        in_specs=smem(3) + anyspace(5) + vmem(10),
        out_specs=tuple(vmem(2) + anyspace(2)),
        scratch_shapes=[
            VM((5, TILES, 8, 256), BF16),
            VM((1024, 2304), BF16),
            VM((4, 128, 256), F32),
            VM((4, 128, 256), F32),
            VM((1024, 256), F32),
            VM((2, 528, 512), BF16),
            pltpu.SemaphoreType.DMA((7,)),
        ],
        cost_estimate=cost(2 * 1024 * 2304 * 256, 8 << 20, 1 << 18),
    )(index, occ, core, *stores, xb, acc, band, band_z, bias, pool, pick, latent, proj, gain)


def restore_kernel(blocks, out, turned):
    for g in range(4):
        for half in range(2):
            lanes = slice(128 * half, 128 * half + 128)
            four = [blocks[4 * g + j, :, lanes] for j in range(4)]
            for k, sheet in enumerate(swap_blocks(four)):
                turned[g, pl.ds(4 * half + k, 64, stride=8), :] = sheet
    for g in range(4):
        rows = turned[g].T
        for j in range(4):
            out[4 * g + j] = rows[32 * j : 32 * j + 32].astype(BF16)


def restore(blocks):
    return pl.pallas_call(
        restore_kernel,
        name="restore",
        out_shape=jax.ShapeDtypeStruct((16, 32, 512), BF16),
        in_specs=vmem(1),
        out_specs=vmem(1)[0],
        scratch_shapes=[VM((4, 512, 128), F32)],
        cost_estimate=cost(1 << 20, 2 << 20),
    )(blocks)


NT = (((1,), (1,)), ((), ()))
SCALE = HD ** (-0.5) * math.log2(math.e)


def column_max(part):
    return jnp.max(part, axis=0, keepdims=True)


def own_kernel(
    occ, core, to_partner, to_cross, wq, wk, wv_t, query, state, peak, normed, keys, values, sems
):
    copies = [
        pltpu.make_async_copy(
            to_partner.at[pl.ds(0, 512)], normed.at[1 - core[0]], sems.at[0]
        ),
        pltpu.make_async_copy(to_cross.at[pl.ds(0, 512)], normed.at[core[0]], sems.at[1]),
    ]
    for copy in copies:
        copy.start()
    for copy in copies:
        copy.wait()
    lane = lax.broadcasted_iota(jnp.int32, (512, 128), 1)
    for half in range(2):
        rows = normed[half]
        found = jnp.dot(rows, wq[...], preferred_element_type=F32) * SCALE
        for head in range(8):
            pair = found[:, 128 * (head // 2) : 128 * (head // 2) + 128]
            keep = lane < 64 if head % 2 == 0 else lane >= 64
            query[head, half] = jnp.where(keep, pair, 0.0).astype(BF16)
        found = jnp.dot(rows, wk[...], preferred_element_type=F32)
        for pair in range(4):
            keys[pair, half] = found[:, 128 * pair : 128 * pair + 128].astype(BF16)
        found = lax.dot_general(wv_t[...], rows, NT, preferred_element_type=F32)
        for head in range(8):
            values[head, half, 0:64, :] = found[64 * head : 64 * head + 64].astype(BF16)
            values[head, half, 64:80, :] = jnp.ones((16, 512), BF16)

    row = lax.broadcasted_iota(jnp.int32, (128, 128), 0)
    col = lax.broadcasted_iota(jnp.int32, (128, 128), 1)
    eye = row == col

    def per_head(head, carry):
        for half in range(2):
            bias = [
                jnp.where(occ[8 * half + b] > 0, 0.0, NEG).astype(F32) for b in range(8)
            ]
            for tile in range(2):
                lanes = slice(256 * tile, 256 * tile + 256)
                scores = lax.dot_general(
                    keys[head // 2, half],
                    query[head, half, lanes, :],
                    NT,
                    preferred_element_type=F32,
                )
                top = None
                for b in range(8):
                    part = scores[64 * b : 64 * b + 8]
                    for k in range(1, 8):
                        part = jnp.maximum(part, scores[64 * b + 8 * k : 64 * b + 8 * k + 8])
                    part = part + bias[b]
                    top = part if top is None else jnp.maximum(top, part)
                top = column_max(top)
                selves, dead = [], []
                for k in range(2):
                    first = 256 * tile + 128 * k
                    block = scores[first : first + 128, 128 * k : 128 * k + 128]
                    selves.append(column_max(jnp.where(eye, block, NEG)))
                    brick = first // 64
                    one = lax.broadcasted_iota(jnp.int32, (1, 128), 1)
                    dead.append(jnp.where(one < 64, bias[brick], bias[brick + 1]))
                own = jnp.concatenate(selves, axis=1)
                dead = jnp.concatenate(dead, axis=1)
                own = jnp.where(dead < 0.0, own, NEG)
                top = jnp.maximum(top, own)
                parts = []
                for b in range(8):
                    parts.append(
                        jnp.exp2(scores[64 * b : 64 * b + 64] - (top - bias[b])).astype(BF16)
                    )
                weights = jnp.concatenate(parts, axis=0)
                out = jnp.dot(values[head, half], weights, preferred_element_type=F32)
                extra = jnp.where(dead < 0.0, jnp.exp2(own - top), 0.0)
                out = out + extra * values[head, half, :, lanes].astype(F32)
                state[head, half, :, lanes] = out[0:72]
                peak[head, half, :, lanes] = jnp.broadcast_to(top, (8, 256))
        return carry

    lax.fori_loop(0, 8, per_head, 0)


def own_attention(occ, core, to_partner, to_cross, wq, wk, wv_t):
    return pl.pallas_call(
        own_kernel,
        name="own_attention",
        out_shape=(
            jax.ShapeDtypeStruct((8, 2, 512, 128), BF16),
            jax.ShapeDtypeStruct((8, 2, 72, 512), F32),
            jax.ShapeDtypeStruct((8, 2, 8, 512), F32),
        ),
        in_specs=smem(2) + anyspace(2) + vmem(3),
        out_specs=tuple(vmem(3)),
        scratch_shapes=[
            VM((2, 512, 512), BF16),
            VM((4, 2, 512, 128), BF16),
            VM((8, 2, 80, 512), BF16),
            pltpu.SemaphoreType.DMA((2,)),
        ],
        cost_estimate=cost(6 << 30, 8 << 20, 1 << 22),
    )(occ, core, to_partner, to_cross, wq, wk, wv_t)


def side_kernel(
    half_ref, remote, query, state, peak, wk, wv_t, wo_t, latent_t, proj_t, pooled, *rest
):
    if len(rest) == 7:
        other, out, keys, values, attended, spare, sems = rest
    else:
        out, keys, values, attended, sems = rest
    half = half_ref[0]
    rows = remote[0:512, :]
    found = jnp.dot(rows, wk[...], preferred_element_type=F32)
    for pair in range(4):
        keys[pair] = found[:, 128 * pair : 128 * pair + 128].astype(BF16)
    found = lax.dot_general(wv_t[...], rows, NT, preferred_element_type=F32)
    for head in range(8):
        values[head, 0:64, :] = found[64 * head : 64 * head + 64].astype(BF16)
        values[head, 64:80, :] = jnp.ones((16, 512), BF16)
    flags = remote[512:528, :].astype(F32)
    biases = [jnp.where(flags[b : b + 1, 0:256] > 0.5, 0.0, NEG) for b in range(8)]

    def per_head(head, carry):
        for tile in range(2):
            lanes = slice(256 * tile, 256 * tile + 256)
            scores = lax.dot_general(
                keys[head // 2], query[head, half, lanes, :], NT, preferred_element_type=F32
            )
            top = None
            for b in range(8):
                part = scores[64 * b : 64 * b + 8]
                for k in range(1, 8):
                    part = jnp.maximum(part, scores[64 * b + 8 * k : 64 * b + 8 * k + 8])
                part = part + biases[b]
                top = part if top is None else jnp.maximum(top, part)
            before = peak[head, half, 0:1, lanes]
            top = jnp.maximum(column_max(top), before)
            parts = []
            for b in range(8):
                parts.append(
                    jnp.exp2(scores[64 * b : 64 * b + 64] - (top - biases[b])).astype(BF16)
                )
            weights = jnp.concatenate(parts, axis=0)
            total = jnp.dot(values[head], weights, preferred_element_type=F32)[0:72]
            total = total + state[head, half, :, lanes] * jnp.exp2(before - top)
            result = total[0:64] / total[64:65]
            attended[pl.ds(pl.multiple_of(head * 64, 64), 64), lanes] = result.astype(BF16)
        return carry

    lax.fori_loop(0, 8, per_head, 0)
    place = pl.ds(pl.multiple_of(half * 512, 512), 512)
    mixing = jnp.dot(wo_t[...], attended[...], preferred_element_type=F32)
    lifted = lax.dot_general(proj_t[...], pooled[place, :], NT, preferred_element_type=F32)
    result = ((latent_t[:, place].astype(F32) + lifted) + mixing).astype(BF16)
    if len(rest) == 7:
        out[:, place] = result
        out[:, pl.ds(pl.multiple_of((1 - half) * 512, 512), 512)] = other[...]
    else:
        out[...] = result


def side_attention(half, remote, query, state, peak, wk, wv_t, wo_t, latent_t, proj_t, pooled, other):
    last = other is not None
    return pl.pallas_call(
        side_kernel,
        name="last_attention" if last else "side_attention",
        out_shape=jax.ShapeDtypeStruct((512, 1024 if last else 512), BF16),
        in_specs=smem(1) + vmem(11 if last else 10),
        out_specs=vmem(1)[0],
        scratch_shapes=[
            VM((4, 512, 128), BF16),
            VM((8, 80, 512), BF16),
            VM((512, 512), BF16),
        ]
        + ([VM((8, 128), F32)] if last else [])
        + [pltpu.SemaphoreType.DMA((1,))],
        cost_estimate=cost(4 << 30, 6 << 20, 1 << 21),
    )(
        half, remote, query, state, peak, wk, wv_t, wo_t, latent_t, proj_t, pooled,
        *([other] if last else []),
    )


def pool_tables():
    pool = np.zeros((64, 64), np.float32)
    pick = np.zeros((64, 256), np.float32)
    for token in range(64):
        p = (token // 32) * 2 + token // 4 % 2
        q = (token // 16 % 2) * 2 + token // 2 % 2
        r = (token // 8 % 2) * 2 + token % 2
        for x in (2 * p, 2 * p + 1):
            for y in (2 * q, 2 * q + 1):
                pool[token, 8 * x + y] = 0.125
        pick[token, 64 * r : 64 * r + 64] = 1.0
    return jnp.asarray(pool, BF16), jnp.asarray(pick, F32)


def moved(array, by):
    size = lax.axis_size(AXES)
    pairs = [(i, i + by) for i in range(size) if 0 <= i + by < size]
    return lax.ppermute(array, AXES, pairs)


def swapped(array):
    size = lax.axis_size(AXES)
    return lax.ppermute(array, AXES, [(i, i ^ 1) for i in range(size)])


def crossed(array):
    size = lax.axis_size(AXES)
    pairs = [(i, (i - 1) % size if i % 2 == 0 else (i + 1) % size) for i in range(size)]
    return lax.ppermute(array, AXES, pairs)


def local(
    features, occupancy, neighbours, conv_weight, conv_bias, latent, token_proj, norm_gain,
    qkv_weight, out_weight,
):
    me = lax.axis_index(AXES)
    core = me % 2
    count = features.shape[0]
    xb, faces = prep(occupancy, features)
    back = moved(faces, 2)
    ahead = moved(faces, -2)
    partner = swapped(faces)
    relay = swapped(jnp.where(core == 1, back, ahead))
    (
        conv_weight, conv_bias, latent_in, token_proj, qkv_weight, out_weight, neighbours, _
    ) = lax.optimization_barrier(
        (conv_weight, conv_bias, latent, token_proj, qkv_weight, out_weight, neighbours, faces)
    )
    band, band_z = bands(conv_weight)
    bias = jnp.tile(conv_bias, 8)[None, :]
    pool, pick = pool_tables()
    proj = jnp.pad(token_proj, ((0, 96), (0, 0)))
    proj_t = proj.T
    wq, wk = qkv_weight[0], qkv_weight[1]
    wv_t, wo_t = qkv_weight[2].T, out_weight.T
    latent_t = latent_in.T
    has_peer = neighbours >= 0
    peer = jnp.where(has_peer, neighbours, 0)
    away = jnp.clip(peer // count - me, -REACH, REACH)
    slots = jnp.where(core == 0, jnp.array([1, 4, 0, 3, 2]), jnp.array([1, 3, 0, 4, 2]))
    slot = jnp.zeros_like(away)
    for spread in range(-REACH, REACH + 1):
        slot = jnp.where(away == spread, slots[spread + REACH], slot)
    index = jnp.where(has_peer, slot * count + peer % count, -1).reshape(-1).astype(jnp.int32)
    core_ref = core.astype(jnp.int32).reshape(1)

    acc = inner(xb, band)
    blocks, pooled, to_partner, to_cross = outer(
        index, occupancy, core_ref, (faces, back, ahead, partner, relay), xb, acc, band, band_z,
        bias, pool, pick, latent, proj, norm_gain[None, :],
    )
    from_cross = crossed(to_cross)
    from_partner = swapped(to_partner)
    query, state, peak = own_attention(occupancy, core_ref, to_partner, to_cross, wq, wk, wv_t)
    conv_out = restore(blocks)
    shared = (query, state, peak, wk, wv_t, wo_t, latent_t, proj_t, pooled)
    first = side_attention(1 - core_ref, from_partner, *shared, None)
    tokens_out = side_attention(core_ref, from_cross, *shared, first)
    return (conv_out, tokens_out)


def solution(mesh):
    return jax.shard_map(
        local,
        mesh=mesh,
        in_specs=(
            P(AXES, None, None),
            P(AXES),
            P(AXES, None),
            P(),
            P(),
            P(AXES, None),
            P(),
            P(),
            P(),
            P(),
        ),
        out_specs=(P(AXES, None, None), P(None, AXES)),
        check_vma=False,
    )
```

time: 166 us -> 111 us (0.67)
  the two profiles are of different devices: /device:TPU:15 before, /device:TPU:1 now
where the time goes in v1:
time: 111 us; the launch traced here: 110 us
  Pallas kernels  74.9 us (67%)
  local copies, waits for them, and re-layouts  14.1 us (13%)
  starting transfers between devices  13.4 us (12%)
  other arithmetic  4.75 us (4%)
  waiting for transfers between devices  2.35 us (2%)
    pallas_call x2, Pallas kernels, side_attention(): pl.pallas_call(side_kernel, name='last_attention' if last else 'side_atte...  25.6 us
    pallas_call x1, Pallas kernels, own_attention(): pl.pallas_call(own_kernel, name='own_attention', out_shape=(jax.ShapeDtyp...  19.6 us
    pallas_call x1, Pallas kernels, outer(): pl.pallas_call(outer_kernel, name='outer', out_shape=(jax.ShapeDtypeStruc...  15.4 us
    ppermute x3, starting transfers between devices, swapped(): return lax.ppermute(array, AXES, [(i, i ^ 1) for i in range(size)])  6.06 us
    optimization_barrier x4, local copies, waits for them, and re-layouts, local(): lax.optimization_barrier((conv_weight, conv_bias, latent, token_proj, qkv...  5.33 us
    ppermute x2, starting transfers between devices, moved(): return lax.ppermute(array, AXES, pairs)  5.27 us
    pallas_call x1, Pallas kernels, inner(): pl.pallas_call(inner_kernel, name='inner', out_shape=jax.ShapeDtypeStruct...  4.49 us
    pallas_call x1, Pallas kernels, prep(): pl.pallas_call(prep_kernel, name='prep', out_shape=(jax.ShapeDtypeStruct(...  3.57 us
  transfers between devices with their start and end apart: 6, of which 1 were waited for; matrix products, arithmetic and copies ran while one was open for 16% of the time, Pallas kernels for 39%

profile of v1, /device:TPU:1, one launch (start us, length us, event | category | flops | bytes accessed | tf_op | source)
XLA Modules:
  0.0 110.2 jit_solution(8531724368900823693)
XLA Ops:
  0.6 3.6 %prep.1 = (f32[16,64,256]{2,1,0:T(8,128)}, bf16[96,8,256]{2,1,0:T(8,128)(2,1)}) custom-call(s32[16]{0:T(128)} %occ.5, bf16[16,32,512]{2,1,0:T(8,128)(2,1)} %feat.1), custom_call_target="tpu_custom_call" | custom-call | flops 1048576 | bytes 2097152 | tf_op jit(solution)/shard_map/prep/pallas_call | solution.py:84
  4.2 4.0 %collective-permute-start = (bf16[96,8,256]{2,1,0:T(8,128)(2,1)}, bf16[96,8,256]{2,1,0:T(8,128)(2,1)S(1)}, u32[]{:S(2)}, u32[]{:S(2)}) collective-permute-start(bf16[96,8,256]{2,1,0:T(8,128)(2,1)} %get-tuple-element.20.own), channel_id=1, source_target_pairs={{0,2},{1,3},{2,4},{3,5},{4,6},{5,7},{6,8},{7,9},{8,10},{9,11},{10,... | collective-permute-start | bytes 1179656 | tf_op jit(solution)/shard_map/ppermute | solution.py:565
  8.2 1.3 %collective-permute-start.1 = (bf16[96,8,256]{2,1,0:T(8,128)(2,1)}, bf16[96,8,256]{2,1,0:T(8,128)(2,1)S(1)}, u32[]{:S(2)}, u32[]{:S(2)}) collective-permute-start(bf16[96,8,256]{2,1,0:T(8,128)(2,1)} %get-tuple-element.20.own), channel_id=1, source_target_pairs={{2,0},{3,1},{4,2},{5,3},{6,4},{7,5},{8,6},{9,7},{10,8},{11,9},{12,... | collective-permute-start | bytes 1179656 | tf_op jit(solution)/shard_map/ppermute | solution.py:565
  9.5 1.0 collective-permute-start.2
  10.5 0.7 broadcast_select_fusion.1
  11.2 0.7 fusion.4
  11.8 1.7 %copy.25 = bf16[27,32,32]{2,1,0:T(8,128)(2,1)} copy(bf16[27,32,32]{1,2,0:T(8,128)(2,1)} %bitcast.26) | data formatting | bytes 110592 | tf_op jit(solution)/shard_map/transpose | solution.py:144
  13.6 0.0 copy-start.5
  13.6 1.7 %copy.28 = bf16[3,512,512]{1,2,0:T(8,128)(2,1)S(1)} copy(bf16[3,512,512]{2,1,0:T(8,128)(2,1)} %param.23) | data formatting | bytes 3145728 | tf_op jit(solution)/shard_map/optimization_barrier | solution.py:593
  15.3 3.0 %bands.1 = (bf16[2304,256]{1,0:T(8,128)(2,1)}, bf16[2304,256]{1,0:T(8,128)(2,1)}) custom-call(bf16[864,32]{1,0:T(8,128)(2,1)} %bitcast.23, bf16[32,256]{1,0:T(8,128)(2,1)} %constant.74.clone.spread), custom_call_target="tpu_custom_call" | custom-call | flops 16777216 | bytes 3145728 | tf_op jit(solution)/shard_map/bands/pallas_call | solution.py:146
  18.3 0.0 copy-done.5
  18.3 3.2 %compare_select_fusion = s32[16,6]{0,1:T(8,128)S(1)} fusion(s32[16,6]{0,1:T(8,128)S(1)} %copy-done.5, s32[]{:T(128)} %bitcast.4, s32[]{:T(128)} %bitcast.3, s32[]{:T(128)} %bitcast.2, s32[]{:T(128)} %bitcast.1, s32[]{:T(128)} %bitcast, s32[]{:T(128)S(6)} %add.19), kind=kLoop, calls=%fused_computation.9 | loop fusion | flops 3456 | bytes 792 | tf_op jit(solution)/shard_map/jit(_where)/select_n | solution.py:611
  21.5 0.8 slice_bitcast_fusion.wv_t
  22.3 2.3 %collective-permute-done.back = bf16[96,8,256]{2,1,0:T(8,128)(2,1)S(1)} collective-permute-done((bf16[96,8,256]{2,1,0:T(8,128)(2,1)}, bf16[96,8,256]{2,1,0:T(8,128)(2,1)S(1)}, u32[]{:S(2)}, u32[]{:S(2)}) %collective-permute-start) | collective-permute-done | bytes 393248 | tf_op jit(solution)/shard_map/ppermute | solution.py:565
  24.7 0.0 copy-start.2
  24.7 0.0 collective-permute-done.1.ahead
  24.7 0.0 copy-start.3
  24.7 0.9 broadcast_select_fusion
  25.6 1.5 %collective-permute-start.3 = (bf16[96,8,256]{2,1,0:T(8,128)(2,1)}, bf16[96,8,256]{2,1,0:T(8,128)(2,1)}, u32[]{:S(2)}, u32[]{:S(2)}) collective-permute-start(bf16[96,8,256]{2,1,0:T(8,128)(2,1)} %broadcast_select_fusion), channel_id=1, source_target_pairs={{0,1},{1,0},{2,3},{3,2},{4,5},{5,4},{6,7},{7,6},{8,9},{9,8},{10,11... | collective-permute-start | bytes 1179656 | tf_op jit(solution)/shard_map/ppermute | solution.py:570
  27.1 0.0 copy-start.6
  27.1 0.0 copy-start.4
  27.1 4.5 %inner.1.acc = f32[1024,256]{1,0:T(8,128)} custom-call(f32[16,64,256]{2,1,0:T(8,128)} %get-tuple-element.22.xb, bf16[2304,256]{1,0:T(8,128)(2,1)} %get-tuple-element.24.band), custom_call_target="tpu_custom_call" | custom-call | flops 1207959552 | bytes 4194304 | tf_op jit(solution)/shard_map/inner/pallas_call | solution.py:176
  31.6 0.0 copy-done.2
  31.6 0.0 copy-done.3
  31.6 0.0 copy-start.1
  31.6 0.1 copy.24
  31.7 0.6 reshape.14.index
  32.3 0.0 copy-done.6
  32.3 0.7 broadcast_in_dim_tile.3.bias
  33.0 0.0 copy-done.4
  33.0 0.1 copy.26
  33.1 0.1 copy.31
  33.2 0.0 copy-start
  33.2 2.2 %copy.29 = bf16[512,512]{0,1:T(8,128)(2,1)} copy(bf16[512,512]{1,0:T(8,128)(2,1)} %param.24) | data formatting | bytes 1048576 | tf_op jit(solution)/shard_map/optimization_barrier | solution.py:593
  35.4 0.0 copy-done.1
  35.4 1.3 %copy.30 = bf16[1024,512]{0,1:T(8,128)(2,1)} copy(bf16[1024,512]{1,0:T(8,128)(2,1)S(1)} %copy-done.1) | data formatting | bytes 2097152 | tf_op jit(solution)/shard_map/optimization_barrier | solution.py:593
  36.7 0.7 pad.4.clone.proj
  37.4 0.7 pad_bitcast_fusion.proj_t
  38.0 0.0 copy-done
  38.0 1.0 slice_bitcast_fusion.1
  39.1 0.0 collective-permute-done.2.partner
  39.1 0.0 collective-permute-done.3.relay
  39.1 15.4 %outer.1 = (f32[16,64,256]{2,1,0:T(8,128)}, bf16[1024,128]{1,0:T(8,128)(2,1)}, bf16[528,512]{1,0:T(8,128)(2,1)}, bf16[528,512]{1,0:T(8,128)(2,1)}) custom-call(s32[96]{0:T(128)} %reshape.14.index, s32[16]{0:T(128)} %occ.5, s32[1]{0:T(128)} %bitcast.5.core.half_ref, bf16[96,8,256]{2,1,0:T(8,128)(2,1)} %get-tuple-element.20.own, ...), custom_call_target="tpu_custom_call" | custom-call | flops 1207959552 | bytes 8388608 | tf_op jit(solution)/shard_map/outer/pallas_call | solution.py:308
  54.5 2.1 %collective-permute-start.4 = (bf16[528,512]{1,0:T(8,128)(2,1)}, bf16[528,512]{1,0:T(8,128)(2,1)S(1)}, u32[]{:S(2)}, u32[]{:S(2)}) collective-permute-start(bf16[528,512]{1,0:T(8,128)(2,1)} %get-tuple-element.29.to_cross), channel_id=1, source_target_pairs={{0,31},{1,2},{2,1},{3,4},{4,3},{5,6},{6,5},{7,8},{8,7},{9,10},{10,... | collective-permute-start | bytes 1622024 | tf_op jit(solution)/shard_map/ppermute | solution.py:576
  56.6 3.5 %collective-permute-start.5 = (bf16[528,512]{1,0:T(8,128)(2,1)}, bf16[528,512]{1,0:T(8,128)(2,1)S(1)}, u32[]{:S(2)}, u32[]{:S(2)}) collective-permute-start(bf16[528,512]{1,0:T(8,128)(2,1)} %get-tuple-element.30.to_partner), channel_id=1, source_target_pairs={{0,1},{1,0},{2,3},{3,2},{4,5},{5,4},{6,7},{7,6},{8,9},{9,8},{10,11... | collective-permute-start | bytes 1622024 | tf_op jit(solution)/shard_map/ppermute | solution.py:570
  60.1 19.6 %own_attention.1 = (bf16[8,2,512,128]{3,2,1,0:T(8,128)(2,1)}, f32[8,2,72,512]{3,2,1,0:T(8,128)}, f32[8,2,8,512]{3,2,1,0:T(8,128)}) custom-call(s32[16]{0:T(128)} %occ.5, s32[1]{0:T(128)} %bitcast.5.core.half_ref, bf16[528,512]{1,0:T(8,128)(2,1)} %get-tuple-element.30.to_partner, bf16[528,512]{1,0:T(8,128)(2,1)} %get-tuple-element.29.to_cross, ...), custom_call_target="tpu_custom_call" | custom-call | flops 6442450944 | bytes 8388608 | tf_op jit(solution)/shard_map/own_attention/pallas_call | solution.py:448
  79.7 3.2 %restore.1 = bf16[16,32,512]{2,1,0:T(8,128)(2,1)} custom-call(f32[16,64,256]{2,1,0:T(8,128)} %get-tuple-element.28.blocks), custom_call_target="tpu_custom_call" | custom-call | flops 1048576 | bytes 2097152 | tf_op jit(solution)/shard_map/restore/pallas_call | solution.py:346
  82.9 0.0 collective-permute-done.5.remote
  82.9 0.0 copy-start.8
  82.9 0.8 copy-done.8
  83.7 12.6 %side_attention.1.rest_0_ = bf16[512,512]{1,0:T(8,128)(2,1)} custom-call(s32[1]{0:T(128)S(6)} %sub.18.half_ref, bf16[528,512]{1,0:T(8,128)(2,1)} %copy-done.8, bf16[8,2,512,128]{3,2,1,0:T(8,128)(2,1)} %get-tuple-element.32.query, f32[8,2,72,512]{3,2,1,0:T(8,128)} %get-tuple-element.33.state, f32[8,2,8,512]{3,2,1,0:T(8,128)} %get-tuple-element.34.peak, ...), custom_call_target="tpu_custom_call" | custom-call | flops 4294967296 | bytes 6291456 | tf_op jit(solution)/shard_map/side_attention/pallas_call | solution.py:528
  96.3 0.0 collective-permute-done.4.remote
  96.4 0.0 copy-start.7
  96.4 0.8 copy-done.7
  97.2 13.0 %last_attention.1 = bf16[512,1024]{1,0:T(8,128)(2,1)} custom-call(s32[1]{0:T(128)} %bitcast.5.core.half_ref, bf16[528,512]{1,0:T(8,128)(2,1)} %copy-done.7, bf16[8,2,512,128]{3,2,1,0:T(8,128)(2,1)} %get-tuple-element.32.query, f32[8,2,72,512]{3,2,1,0:T(8,128)} %get-tuple-element.33.state, f32[8,2,8,512]{3,2,1,0:T(8,128)} %get-tuple-element.34.peak, ...), custom_call_target="tpu_custom_call" | custom-call | flops 4294967296 | bytes 6291456 | tf_op jit(solution)/shard_map/last_attention/pallas_call | solution.py:528
  (1 shorter events, 0.0 us)
Async XLA Ops:
  4.2 20.5 %collective-permute-start = (bf16[96,8,256]{2,1,0:T(8,128)(2,1)}, bf16[96,8,256]{2,1,0:T(8,128)(2,1)S(1)}, u32[]{:S(2)}, u32[]{:S(2)}) collective-permute-start(bf16[96,8,256]{2,1,0:T(8,128)(2,1)} %get-tuple-element.20.own), channel_id=1, source_target_pairs={{0,2},{1,3},{2,4},{3,5},{4,6},{5,7},{6,8},{7,9},{8,10},{9,11},{10,... | collective-permute-start | bytes 1179656 | tf_op jit(solution)/shard_map/ppermute | solution.py:565
  8.2 16.5 %collective-permute-start.1 = (bf16[96,8,256]{2,1,0:T(8,128)(2,1)}, bf16[96,8,256]{2,1,0:T(8,128)(2,1)S(1)}, u32[]{:S(2)}, u32[]{:S(2)}) collective-permute-start(bf16[96,8,256]{2,1,0:T(8,128)(2,1)} %get-tuple-element.20.own), channel_id=1, source_target_pairs={{2,0},{3,1},{4,2},{5,3},{6,4},{7,5},{8,6},{9,7},{10,8},{11,9},{12,... | collective-permute-start | bytes 1179656 | tf_op jit(solution)/shard_map/ppermute | solution.py:565
  9.5 29.6 %collective-permute-start.2 = (bf16[96,8,256]{2,1,0:T(8,128)(2,1)}, bf16[96,8,256]{2,1,0:T(8,128)(2,1)}, u32[]{:S(2)}, u32[]{:S(2)}) collective-permute-start(bf16[96,8,256]{2,1,0:T(8,128)(2,1)} %get-tuple-element.20.own), channel_id=1, source_target_pairs={{0,1},{1,0},{2,3},{3,2},{4,5},{5,4},{6,7},{7,6},{8,9},{9,8},{10,11... | collective-permute-start | bytes 1179656 | tf_op jit(solution)/shard_map/ppermute | solution.py:570
  13.6 4.7 %copy-start.5 = (s32[16,6]{0,1:T(8,128)S(1)}, s32[16,6]{0,1:T(8,128)}, u32[]{:S(2)}) copy-start(s32[16,6]{0,1:T(8,128)} %param.17) | copy-start | bytes 1156
  24.7 6.9 %copy-start.2 = (bf16[96,8,256]{2,1,0:T(8,128)(2,1)}, bf16[96,8,256]{2,1,0:T(8,128)(2,1)S(1)}, u32[]{:S(2)}) copy-start(bf16[96,8,256]{2,1,0:T(8,128)(2,1)S(1)} %collective-permute-done.back) | copy-start | bytes 1179652
  24.7 6.9 %copy-start.3 = (bf16[96,8,256]{2,1,0:T(8,128)(2,1)}, bf16[96,8,256]{2,1,0:T(8,128)(2,1)S(1)}, u32[]{:S(2)}) copy-start(bf16[96,8,256]{2,1,0:T(8,128)(2,1)S(1)} %collective-permute-done.1.ahead) | copy-start | bytes 1179652
  25.6 13.5 %collective-permute-start.3 = (bf16[96,8,256]{2,1,0:T(8,128)(2,1)}, bf16[96,8,256]{2,1,0:T(8,128)(2,1)}, u32[]{:S(2)}, u32[]{:S(2)}) collective-permute-start(bf16[96,8,256]{2,1,0:T(8,128)(2,1)} %broadcast_select_fusion), channel_id=1, source_target_pairs={{0,1},{1,0},{2,3},{3,2},{4,5},{5,4},{6,7},{7,6},{8,9},{9,8},{10,11... | collective-permute-start | bytes 1179656 | tf_op jit(solution)/shard_map/ppermute | solution.py:570
  27.1 5.2 %copy-start.6 = (f32[32]{0:T(128)S(1)}, f32[32]{0:T(128)}, u32[]{:S(2)}) copy-start(f32[32]{0:T(128)} %param.19) | copy-start | bytes 388
  27.1 5.9 %copy-start.4 = (bf16[32,512]{1,0:T(8,128)(2,1)S(1)}, bf16[32,512]{1,0:T(8,128)(2,1)}, u32[]{:S(2)}) copy-start(bf16[32,512]{1,0:T(8,128)(2,1)} %param.21) | copy-start | bytes 98308
  31.6 3.8 %copy-start.1 = (bf16[1024,512]{1,0:T(8,128)(2,1)S(1)}, bf16[1024,512]{1,0:T(8,128)(2,1)}, u32[]{:S(2)}) copy-start(bf16[1024,512]{1,0:T(8,128)(2,1)} %latent.1) | copy-start | bytes 3145732
  33.2 4.8 %copy-start = (bf16[3,512,512]{2,1,0:T(8,128)(2,1)S(1)}, bf16[3,512,512]{2,1,0:T(8,128)(2,1)}, u32[]{:S(2)}) copy-start(bf16[3,512,512]{2,1,0:T(8,128)(2,1)} %param.23) | copy-start | bytes 4718596
  54.5 41.8 %collective-permute-start.4 = (bf16[528,512]{1,0:T(8,128)(2,1)}, bf16[528,512]{1,0:T(8,128)(2,1)S(1)}, u32[]{:S(2)}, u32[]{:S(2)}) collective-permute-start(bf16[528,512]{1,0:T(8,128)(2,1)} %get-tuple-element.29.to_cross), channel_id=1, source_target_pairs={{0,31},{1,2},{2,1},{3,4},{4,3},{5,6},{6,5},{7,8},{8,7},{9,10},{10,... | collective-permute-start | bytes 1622024 | tf_op jit(solution)/shard_map/ppermute | solution.py:576
  56.6 26.4 %collective-permute-start.5 = (bf16[528,512]{1,0:T(8,128)(2,1)}, bf16[528,512]{1,0:T(8,128)(2,1)S(1)}, u32[]{:S(2)}, u32[]{:S(2)}) collective-permute-start(bf16[528,512]{1,0:T(8,128)(2,1)} %get-tuple-element.30.to_partner), channel_id=1, source_target_pairs={{0,1},{1,0},{2,3},{3,2},{4,5},{5,4},{6,7},{7,6},{8,9},{9,8},{10,11... | collective-permute-start | bytes 1622024 | tf_op jit(solution)/shard_map/ppermute | solution.py:570
  82.9 0.8 copy-start.8
  96.4 0.8 copy-start.7

commit v2 on v1

v2 whole, which is shorter than its diff:
```python
import math

import jax
import jax.numpy as jnp
import numpy as np
from jax import lax
from jax.experimental import pallas as pl
from jax.experimental.pallas import tpu as pltpu
from jax.sharding import PartitionSpec as P

HD = 64
WIN = 1024
REACH = 2
AXES = ("space", "chan")
NEG = -1e30
TILES = 96
F32 = jnp.float32
BF16 = jnp.bfloat16
VM = pltpu.VMEM
NT = (((1,), (1,)), ((), ()))
SCALE = HD ** (-0.5) * math.log2(math.e)
LIMIT = pltpu.CompilerParams(vmem_limit_bytes=20 << 20)


def vmem(count):
    return [pl.BlockSpec(memory_space=pltpu.VMEM)] * count


def smem(count):
    return [pl.BlockSpec(memory_space=pltpu.SMEM)] * count


def anyspace(count):
    return [pl.BlockSpec(memory_space=pl.ANY)] * count


def cost(flops, moved, trans=0):
    return pl.CostEstimate(flops=flops, bytes_accessed=moved, transcendentals=trans)


def swap_blocks(four):
    lane = lax.broadcasted_iota(jnp.int32, four[0].shape, 1)
    low = lane < 64
    even = (lane // 32) % 2 == 0
    half = []
    for a, b in ((0, 2), (1, 3)):
        half.append(jnp.where(low, four[a], pltpu.roll(four[b], 64, 1)))
        half.append(jnp.where(low, pltpu.roll(four[a], 64, 1), four[b]))
    a0, a2, a1, a3 = half
    return [
        jnp.where(even, a0, pltpu.roll(a1, 32, 1)),
        jnp.where(even, pltpu.roll(a0, 96, 1), a1),
        jnp.where(even, a2, pltpu.roll(a3, 32, 1)),
        jnp.where(even, pltpu.roll(a2, 96, 1), a3),
    ]


def lanes_of(half):
    return slice(128 * half, 128 * half + 128)


def prep_kernel(occ, feat, order, xb, faces, masked):
    for b in range(16):
        rows = feat[b].astype(F32) * occ[b].astype(F32)
        masked[32 * b : 32 * b + 32, :] = rows.astype(BF16)
    for two in range(2):
        found = lax.dot_general(
            order[...], masked[256 * two : 256 * two + 256, :], NT, preferred_element_type=F32
        )
        for g in (2 * two, 2 * two + 1):
            sheets = [found[64 * z : 64 * z + 64, lanes_of(g % 2)] for z in range(8)]
            for face, z in ((0, 0), (1, 7)):
                for xq in range(4):
                    tile = jnp.concatenate(
                        [sheets[z][8 * xq : 8 * xq + 8], sheets[z][8 * xq + 32 : 8 * xq + 40]],
                        axis=1,
                    )
                    faces[64 + (2 * g + face) * 4 + xq] = tile.astype(BF16)
            for half in range(2):
                for j, block in enumerate(swap_blocks(sheets[4 * half : 4 * half + 4])):
                    b = 4 * g + j
                    xb[half, b] = block
                    faces[4 * b, :, lanes_of(half)] = block[56:64].astype(BF16)
                    faces[4 * b + 1, :, lanes_of(half)] = block[0:8].astype(BF16)
    for b in range(16):
        for half in range(2):
            for face, y in ((2, 7), (3, 0)):
                sheet = xb[half, b, pl.ds(y, 8, stride=8), :]
                faces[4 * b + face, :, lanes_of(half)] = sheet.astype(BF16)


def prep(occ, feat):
    order = np.zeros((512, 512), np.float32)
    at = np.arange(512)
    order[at, at % 64 * 8 + at // 64] = 1.0
    return pl.pallas_call(
        prep_kernel,
        name="prep",
        out_shape=(
            jax.ShapeDtypeStruct((2, 16, 64, 128), F32),
            jax.ShapeDtypeStruct((TILES, 8, 256), BF16),
        ),
        in_specs=smem(1) + vmem(2),
        out_specs=tuple(vmem(2)),
        scratch_shapes=[VM((512, 512), BF16)],
        compiler_params=LIMIT,
        cost_estimate=cost(1 << 28, 2 << 20),
    )(occ, feat, jnp.asarray(order, BF16))


def shifted_rows(tile, step):
    if step == 0:
        return tile
    row = lax.broadcasted_iota(jnp.int32, tile.shape, 0) % 8
    if step < 0:
        moved = pltpu.roll(tile, 1, 0)
        return jnp.where(row == 0, 0.0, moved)
    moved = pltpu.roll(tile, tile.shape[0] - 1, 0)
    return jnp.where(row == 7, 0.0, moved)


def joined(pair, *at):
    return jnp.concatenate([pair[(0, *at)], pair[(1, *at)]], axis=1)


def write_patches(lhs, brick, tiles):
    zero = jnp.zeros((8, 256), F32)
    rows = pl.ds(pl.multiple_of(brick * 64, 64), 64)
    for dy in (-1, 0, 1):
        moved = [shifted_rows(t, dy) for t in tiles]
        for dx in (-1, 0, 1):
            picked = [moved[x + dx] if 0 <= x + dx < 8 else zero for x in range(8)]
            tap = (dx + 1) * 3 + dy + 1
            lhs[rows, 256 * tap : 256 * tap + 256] = jnp.concatenate(picked, axis=0).astype(BF16)


def turn(eye, array):
    return lax.dot_general(eye, array, NT, preferred_element_type=F32).astype(BF16)


def weights_kernel(
    conv, spread, qkv, out_weight, latent, token_proj,
    band, band_z, wv_t, wo_t, latent_t, proj_t, wide,
):
    for tap in range(27):
        wide[32 * tap : 32 * tap + 32, :] = jnp.dot(
            conv[tap].astype(F32).T.astype(BF16), spread[...], preferred_element_type=F32
        )
    block = lax.broadcasted_iota(jnp.int32, (32, 256), 1) // 32

    def per_tap(t, carry):
        base = [
            wide[pl.ds(pl.multiple_of((t * 3 + k) * 32, 32), 32), :] for k in range(3)
        ]
        for z in range(8):
            value = jnp.where(block == z, base[1], 0.0)
            value = jnp.where(block == z + 1, base[0], value)
            value = jnp.where(block == z - 1, base[2], value)
            band[pl.ds(pl.multiple_of(t * 256 + 32 * z, 32), 32), :] = value.astype(BF16)
        return carry

    lax.fori_loop(0, 9, per_tap, 0)
    for dy in range(3):
        for face, k in ((0, 0), (1, 2)):
            value = jnp.zeros((32, 256), F32)
            for dx in range(3):
                start = ((dx * 3 + dy) * 3 + k) * 32
                value = jnp.where(block == 2 * dx + face, wide[start : start + 32, :], value)
            for j in range(4):
                start = dy * 256 + 128 * face + 32 * j
                band_z[start : start + 32, :] = value.astype(BF16)
    row = lax.broadcasted_iota(jnp.int32, (512, 512), 0)
    col = lax.broadcasted_iota(jnp.int32, (512, 512), 1)
    eye = jnp.where(row == col, 1.0, 0.0).astype(BF16)
    wv_t[...] = turn(eye, qkv[2])
    wo_t[...] = turn(eye, out_weight[...])
    latent_t[...] = turn(eye, latent[...])
    proj_t[...] = turn(
        eye, jnp.concatenate([token_proj[...], jnp.zeros((96, 512), BF16)], axis=0)
    )


def weights(conv_weight, qkv, out_weight, latent, token_proj):
    spread = jnp.asarray(np.tile(np.eye(32, dtype=np.float32), (1, 8)), BF16)
    return pl.pallas_call(
        weights_kernel,
        name="weights",
        out_shape=(
            jax.ShapeDtypeStruct((2304, 256), BF16),
            jax.ShapeDtypeStruct((768, 256), BF16),
            jax.ShapeDtypeStruct((512, 512), BF16),
            jax.ShapeDtypeStruct((512, 512), BF16),
            jax.ShapeDtypeStruct((512, 1024), BF16),
            jax.ShapeDtypeStruct((512, 128), BF16),
        ),
        in_specs=vmem(6),
        out_specs=tuple(vmem(6)),
        scratch_shapes=[VM((864, 256), F32)],
        compiler_params=LIMIT,
        cost_estimate=cost(1 << 31, 8 << 20),
    )(conv_weight, spread, qkv, out_weight, latent, token_proj)


def inner_kernel(xb, band, acc, lhs):
    def per_brick(b, carry):
        write_patches(lhs, b, [joined(xb, b, slice(8 * x, 8 * x + 8)) for x in range(8)])
        return carry

    lax.fori_loop(0, 16, per_brick, 0)

    def per_rows(i, carry):
        rows = pl.ds(pl.multiple_of(i * 512, 512), 512)
        acc[rows, :] = jnp.dot(lhs[rows, :], band[...], preferred_element_type=F32)
        return carry

    lax.fori_loop(0, 2, per_rows, 0)


def inner(xb, band):
    return pl.pallas_call(
        inner_kernel,
        name="inner",
        out_shape=jax.ShapeDtypeStruct((1024, 256), F32),
        in_specs=vmem(2),
        out_specs=vmem(1)[0],
        scratch_shapes=[VM((1024, 2304), BF16)],
        compiler_params=LIMIT,
        cost_estimate=cost(2 * 1024 * 2304 * 256, 4 << 20),
    )(xb, band)


def outer_kernel(
    neighbours, occ, me, own, back, ahead, partner, relay, xb, acc, band, band_z, bias, pool, pick,
    latent, proj, gain,
    blocks, pooled, to_partner, to_cross,
    table, store, lhs, flat, edges, sums, halves, sems,
):
    copies = [
        pltpu.make_async_copy(ref, store.at[slot], sems.at[slot])
        for slot, ref in enumerate((own, back, ahead, partner, relay))
    ]
    for copy in copies:
        copy.start()
    core = me[0] % 2
    for away, slot in enumerate((1, 4 - core, 0, 3 + core, 2)):
        table[away] = slot
    for copy in copies:
        copy.wait()
    lane = lax.broadcasted_iota(jnp.int32, (8, 256), 1) % 128 // 32

    def where_from(b, face):
        peer = neighbours[b, face]
        valid = (peer >= 0).astype(F32)
        peer = jnp.maximum(peer, 0)
        away = jnp.clip(peer // 16 - me[0], -REACH, REACH)
        return table[away + REACH], peer % 16, valid

    def gather(b, carry):
        for face in range(4):
            slot, brick, valid = where_from(b, face)
            tile = store[slot, brick * 4 + face].astype(F32) * valid
            flat[face, pl.ds(pl.multiple_of(b * 8, 8), 8), :] = tile
        low, high = [], []
        for face, into in ((0, low), (1, high)):
            slot, brick, valid = where_from(b, 4 + face)
            base = 64 + (brick // 4 * 2 + (1 - face)) * 4
            mask = jnp.where(lane == brick % 4, valid, 0.0)
            for xq in range(4):
                into.append(store[slot, base + xq].astype(F32) * mask)
        tiles = []
        for x in range(8):
            part = lanes_of(x // 4)
            tiles.append(jnp.concatenate([low[x % 4][:, part], high[x % 4][:, part]], axis=1))
        rows = pl.ds(pl.multiple_of(b * 64, 64), 64)
        for dy in (-1, 0, 1):
            moved = [shifted_rows(t, dy) for t in tiles]
            start = 256 * (dy + 1)
            lhs[rows, start : start + 256] = jnp.concatenate(moved, axis=0).astype(BF16)
        return carry

    lax.fori_loop(0, 16, gather, 0)
    for face in range(4):
        sheet = flat[face]
        side = 0 if face % 2 == 0 else 2
        total = None
        for step in (-1, 0, 1):
            tap = side * 3 + step + 1 if face < 2 else (step + 1) * 3 + side
            part = jnp.dot(
                shifted_rows(sheet, step).astype(BF16),
                band[256 * tap : 256 * tap + 256, :],
                preferred_element_type=F32,
            )
            total = part if total is None else total + part
        edges[face] = total
    for i in range(2):
        rows = slice(512 * i, 512 * i + 512)
        sums[rows, :] = jnp.dot(lhs[rows, :], band_z[...], preferred_element_type=F32)
    row = lax.broadcasted_iota(jnp.int32, (8, 256), 0)
    one = lax.broadcasted_iota(jnp.int32, (8, 128), 1)

    def finish(b, alive):
        start = pl.multiple_of(b * 64, 64)
        sheet_rows = pl.ds(pl.multiple_of(b * 8, 8), 8)
        y_low, y_high = edges[2, sheet_rows, :], edges[3, sheet_rows, :]
        done = []
        for x in range(8):
            tile_rows = pl.ds(start + 8 * x, 8)
            rim = pltpu.roll(sums[tile_rows, 0:128], 64, 1)
            if x > 0:
                rim = rim + sums[pl.ds(start + 8 * x - 8, 8), 0:128]
            if x < 7:
                rim = rim + sums[pl.ds(start + 8 * x + 8, 8), 128:256]
            rim = jnp.concatenate(
                [
                    jnp.where(one < 32, rim, 0.0),
                    jnp.where(one >= 96, pltpu.roll(rim, 64, 1), 0.0),
                ],
                axis=1,
            )
            total = acc[tile_rows, :] + rim
            total = total + jnp.where(row == 0, y_low[x : x + 1, :], 0.0)
            total = total + jnp.where(row == 7, y_high[x : x + 1, :], 0.0)
            if x == 0:
                total = total + edges[0, sheet_rows, :]
            if x == 7:
                total = total + edges[1, sheet_rows, :]
            value = total + bias[...]
            kept = joined(xb, b, slice(8 * x, 8 * x + 8))
            done.append(alive * (kept + value / (1.0 + jnp.exp(-value))))
        block = jnp.concatenate(done, axis=0).astype(BF16)
        for half in range(2):
            blocks[half, b] = block[:, lanes_of(half)].astype(F32)
        cells = jnp.dot(pool[...], block, preferred_element_type=F32) * pick[...]
        cells = cells[:, :128] + cells[:, 128:]
        cells = cells + pltpu.roll(cells, 64, 1)
        cells = cells + pltpu.roll(cells, 32, 1)
        pooled[pl.ds(start, 64), :] = cells.astype(BF16)

    def finish_two(i, carry):
        for k in range(2):
            finish(2 * i + k, occ[2 * i + k].astype(F32))
        return carry

    lax.fori_loop(0, 8, finish_two, 0)

    def norm(i, carry):
        rows = pl.ds(pl.multiple_of(i * 256, 256), 256)
        lifted = jnp.dot(pooled[rows, 0:32], proj[...], preferred_element_type=F32)
        mixed = latent[rows, :].astype(F32) + lifted
        scale = lax.rsqrt(jnp.mean(mixed * mixed, axis=-1, keepdims=True) + 1e-06)
        halves[i // 2, pl.ds(pl.multiple_of(i % 2 * 256, 256), 256), :] = (
            mixed * scale * gain[...]
        ).astype(BF16)
        return carry

    lax.fori_loop(0, 4, norm, 0)
    flag_row = lax.broadcasted_iota(jnp.int32, (16, 512), 0)
    flag_lane = lax.broadcasted_iota(jnp.int32, (16, 512), 1) // 64
    for half in range(2):
        flags = jnp.zeros((16, 512), F32)
        for b in range(8):
            here = (flag_row == 8 + b) | ((flag_row == 0) & (flag_lane == b))
            flags = jnp.where(here, occ[8 * half + b].astype(F32), flags)
        halves[half, 512:528, :] = flags.astype(BF16)
    out = [
        pltpu.make_async_copy(halves.at[1 - core], to_partner, sems.at[5]),
        pltpu.make_async_copy(halves.at[core], to_cross, sems.at[6]),
    ]
    for copy in out:
        copy.start()
    for copy in out:
        copy.wait()


def outer(neighbours, occ, me, stores, xb, acc, band, band_z, bias, latent, proj, gain):
    return pl.pallas_call(
        outer_kernel,
        name="outer",
        out_shape=(
            jax.ShapeDtypeStruct((2, 16, 64, 128), F32),
            jax.ShapeDtypeStruct((1024, 128), BF16),
            jax.ShapeDtypeStruct((528, 512), BF16),
            jax.ShapeDtypeStruct((528, 512), BF16),
        ),
        in_specs=smem(3) + anyspace(5) + vmem(10),
        out_specs=tuple(vmem(2) + anyspace(2)),
        scratch_shapes=[
            pltpu.SMEM((8,), jnp.int32),
            VM((5, TILES, 8, 256), BF16),
            VM((1024, 768), BF16),
            VM((4, 128, 256), F32),
            VM((4, 128, 256), F32),
            VM((1024, 256), F32),
            VM((2, 528, 512), BF16),
            pltpu.SemaphoreType.DMA((7,)),
        ],
        compiler_params=LIMIT,
        cost_estimate=cost(2 * 1024 * 2304 * 256, 8 << 20, 1 << 18),
    )(neighbours, occ, me, *stores, xb, acc, band, band_z, bias, *pool_tables(), latent, proj, gain)


def restore_kernel(blocks, out, turned):
    row = lax.broadcasted_iota(jnp.int32, (128, 128), 0)
    col = lax.broadcasted_iota(jnp.int32, (128, 128), 1)
    eye = jnp.where(row == col, 1.0, 0.0).astype(BF16)
    for g in range(4):
        for half in range(2):
            four = [blocks[half, 4 * g + j] for j in range(4)]
            for k, sheet in enumerate(swap_blocks(four)):
                turned[g, pl.ds(4 * half + k, 64, stride=8), :] = sheet
    for g in range(4):
        rows = turn(eye, turned[g].astype(BF16))
        for j in range(4):
            out[4 * g + j] = rows[32 * j : 32 * j + 32]


def restore(blocks):
    return pl.pallas_call(
        restore_kernel,
        name="restore",
        out_shape=jax.ShapeDtypeStruct((16, 32, 512), BF16),
        in_specs=vmem(1),
        out_specs=vmem(1)[0],
        scratch_shapes=[VM((4, 512, 128), F32)],
        compiler_params=LIMIT,
        cost_estimate=cost(1 << 20, 2 << 20),
    )(blocks)


def column_max(part):
    return jnp.max(part, axis=0, keepdims=True)


def largest_norm(array):
    row = lax.broadcasted_iota(jnp.int32, (512, 128), 0) // 64
    col = lax.broadcasted_iota(jnp.int32, (512, 128), 1)
    heads = jnp.where(row == col, 1.0, 0.0).astype(BF16)
    return jnp.max(jnp.dot((array * array).astype(BF16), heads, preferred_element_type=F32))


def bounded(query_norm, key_norm, value_peak):
    return (query_norm * key_norm < 3300.0) & (value_peak < 1e12)


def block_max(scores, biases):
    top = None
    for b in range(8):
        part = scores[64 * b : 64 * b + 8]
        for k in range(1, 8):
            part = jnp.maximum(part, scores[64 * b + 8 * k : 64 * b + 8 * k + 8])
        part = part + biases[b]
        top = part if top is None else jnp.maximum(top, part)
    return column_max(top)


def shifted_weights(scores, top, biases):
    parts = [
        jnp.exp2(scores[64 * b : 64 * b + 64] - (top - biases[b])).astype(BF16) for b in range(8)
    ]
    return jnp.concatenate(parts, axis=0)


def keys_values(rows, wk, wv_t, alive, keys, values, raw):
    found = jnp.dot(rows, wk, preferred_element_type=F32)
    for pair in range(4):
        keys[pair] = found[:, 128 * pair : 128 * pair + 128].astype(BF16)
    key_norm = largest_norm(found)
    found = lax.dot_general(wv_t, rows, NT, preferred_element_type=F32)
    ones = jnp.ones((16, 512), F32)
    for head in range(8):
        block = found[64 * head : 64 * head + 64]
        if raw is not None:
            raw[head, 0:64, :] = block.astype(BF16)
            raw[head, 64:80, :] = ones.astype(BF16)
        values[head, 0:64, :] = (block * alive).astype(BF16)
        values[head, 64:80, :] = (ones * alive).astype(BF16)
    return key_norm, jnp.max(jnp.abs(found))


def own_kernel(
    occ, me, to_partner, to_cross, qkv, wv_t, query, state, peak, stats,
    normed, keys, values, raw, sems,
):
    core = me[0] % 2
    copies = [
        pltpu.make_async_copy(to_partner, normed.at[1 - core], sems.at[0]),
        pltpu.make_async_copy(to_cross, normed.at[core], sems.at[1]),
    ]
    for copy in copies:
        copy.start()
    for copy in copies:
        copy.wait()
    lane = lax.broadcasted_iota(jnp.int32, (512, 128), 1)
    alive = [normed[half, 512:528, :].astype(F32)[0:1] for half in range(2)]
    norms, tops = [], []
    for half in range(2):
        rows = normed[half, 0:512, :]
        found = jnp.dot(rows, qkv[0], preferred_element_type=F32) * SCALE
        norms.append(largest_norm(found))
        for head in range(8):
            pair = found[:, 128 * (head // 2) : 128 * (head // 2) + 128]
            keep = lane < 64 if head % 2 == 0 else lane >= 64
            query[head, half] = jnp.where(keep, pair, 0.0).astype(BF16)
        tops.append(
            keys_values(
                rows, qkv[1], wv_t[...], alive[half], keys.at[half], values.at[half], raw.at[half]
            )
        )
    query_norm = jnp.maximum(norms[0], norms[1])
    key_norm = jnp.maximum(tops[0][0], tops[1][0])
    fast = bounded(query_norm, key_norm, jnp.maximum(tops[0][1], tops[1][1]))
    stats[0] = query_norm
    stats[1] = fast.astype(F32)
    row = lax.broadcasted_iota(jnp.int32, (128, 128), 0)
    col = lax.broadcasted_iota(jnp.int32, (128, 128), 1)
    eye = row == col

    @pl.when(fast)
    def plain():
        def per_head(head, carry):
            for half in range(2):
                for tile in range(2):
                    lanes = slice(256 * tile, 256 * tile + 256)
                    parts, own = [], []
                    for chunk in range(2):
                        scores = lax.dot_general(
                            keys[half, head // 2, 256 * chunk : 256 * chunk + 256, :],
                            query[head, half, lanes, :],
                            NT,
                            preferred_element_type=F32,
                        )
                        weights = jnp.exp2(scores)
                        if chunk == tile:
                            for k in (0, 128):
                                block = weights[k : k + 128, k : k + 128]
                                own.append(
                                    jnp.sum(jnp.where(eye, block, 0.0), axis=0, keepdims=True)
                                )
                        parts.append(weights.astype(BF16))
                    out = jnp.dot(
                        values[half, head],
                        jnp.concatenate(parts, axis=0),
                        preferred_element_type=F32,
                    )
                    extra = jnp.concatenate(own, axis=1) * (1.0 - alive[half][:, lanes])
                    out = out + extra * raw[half, head, :, lanes].astype(F32)
                    state[head, half, :, lanes] = out[0:72]
                    peak[head, half, :, lanes] = jnp.zeros((8, 256), F32)
            return carry

        lax.fori_loop(0, 8, per_head, 0)

    @pl.when(jnp.logical_not(fast))
    def general():
        def per_head(head, carry):
            for half in range(2):
                biases = [
                    jnp.where(occ[8 * half + b] > 0, 0.0, NEG).astype(F32) for b in range(8)
                ]
                for tile in range(2):
                    lanes = slice(256 * tile, 256 * tile + 256)
                    scores = lax.dot_general(
                        keys[half, head // 2],
                        query[head, half, lanes, :],
                        NT,
                        preferred_element_type=F32,
                    )
                    selves = []
                    for k in range(2):
                        first = 256 * tile + 128 * k
                        block = scores[first : first + 128, 128 * k : 128 * k + 128]
                        selves.append(column_max(jnp.where(eye, block, NEG)))
                    dead = alive[half][:, lanes] < 0.5
                    own = jnp.where(dead, jnp.concatenate(selves, axis=1), NEG)
                    top = jnp.maximum(block_max(scores, biases), own)
                    out = jnp.dot(
                        values[half, head],
                        shifted_weights(scores, top, biases),
                        preferred_element_type=F32,
                    )
                    extra = jnp.where(dead, jnp.exp2(own - top), 0.0)
                    out = out + extra * raw[half, head, :, lanes].astype(F32)
                    state[head, half, :, lanes] = out[0:72]
                    peak[head, half, :, lanes] = jnp.broadcast_to(top, (8, 256))
            return carry

        lax.fori_loop(0, 8, per_head, 0)


def own_attention(occ, me, to_partner, to_cross, qkv, wv_t):
    return pl.pallas_call(
        own_kernel,
        name="own_attention",
        out_shape=(
            jax.ShapeDtypeStruct((8, 2, 512, 128), BF16),
            jax.ShapeDtypeStruct((8, 2, 72, 512), F32),
            jax.ShapeDtypeStruct((8, 2, 8, 512), F32),
            jax.ShapeDtypeStruct((8,), F32),
        ),
        in_specs=smem(2) + anyspace(2) + vmem(2),
        out_specs=tuple(vmem(3) + smem(1)),
        scratch_shapes=[
            VM((2, 528, 512), BF16),
            VM((2, 4, 512, 128), BF16),
            VM((2, 8, 80, 512), BF16),
            VM((2, 8, 80, 512), BF16),
            pltpu.SemaphoreType.DMA((2,)),
        ],
        compiler_params=LIMIT,
        cost_estimate=cost(6 << 30, 8 << 20, 1 << 22),
    )(occ, me, to_partner, to_cross, qkv, wv_t)


def side_kernel(
    me, stats, remote, query, state, peak, qkv, wv_t, wo_t, latent_t, proj_t, pooled, *rest
):
    last = len(rest) == 5
    if last:
        other, out, keys, values, attended = rest
        half = me[0] % 2
    else:
        out, keys, values, attended = rest
        half = 1 - me[0] % 2
    flags = remote[512:528, :].astype(F32)
    key_norm, value_peak = keys_values(
        remote[0:512, :], qkv[1], wv_t[...], flags[0:1], keys, values, None
    )
    fast = bounded(stats[0], key_norm, value_peak) & (stats[1] > 0.5)

    def finish(head, lanes, total):
        result = total[0:64] / total[64:65]
        attended[pl.ds(pl.multiple_of(head * 64, 64), 64), lanes] = result.astype(BF16)

    @pl.when(fast)
    def plain():
        def per_two(i, carry):
            for head in (2 * i, 2 * i + 1):
                for tile in range(2):
                    lanes = slice(256 * tile, 256 * tile + 256)
                    parts = []
                    for chunk in range(2):
                        scores = lax.dot_general(
                            keys[i, 256 * chunk : 256 * chunk + 256, :],
                            query[head, half, lanes, :],
                            NT,
                            preferred_element_type=F32,
                        )
                        parts.append(jnp.exp2(scores).astype(BF16))
                    total = jnp.dot(
                        values[head], jnp.concatenate(parts, axis=0), preferred_element_type=F32
                    )
                    finish(head, lanes, total[0:72] + state[head, half, :, lanes])
            return carry

        lax.fori_loop(0, 4, per_two, 0)

    @pl.when(jnp.logical_not(fast))
    def general():
        biases = [jnp.where(flags[8 + b : 9 + b, 0:256] > 0.5, 0.0, NEG) for b in range(8)]

        def per_head(head, carry):
            for tile in range(2):
                lanes = slice(256 * tile, 256 * tile + 256)
                scores = lax.dot_general(
                    keys[head // 2], query[head, half, lanes, :], NT, preferred_element_type=F32
                )
                before = peak[head, half, 0:1, lanes]
                top = jnp.maximum(block_max(scores, biases), before)
                total = jnp.dot(
                    values[head], shifted_weights(scores, top, biases), preferred_element_type=F32
                )
                finish(
                    head, lanes, total[0:72] + state[head, half, :, lanes] * jnp.exp2(before - top)
                )
            return carry

        lax.fori_loop(0, 8, per_head, 0)

    place = pl.ds(pl.multiple_of(half * 512, 512), 512)
    mixing = jnp.dot(wo_t[...], attended[...], preferred_element_type=F32)
    lifted = lax.dot_general(proj_t[...], pooled[place, :], NT, preferred_element_type=F32)
    result = ((latent_t[:, place].astype(F32) + lifted) + mixing).astype(BF16)
    if last:
        out[:, place] = result
        out[:, pl.ds(pl.multiple_of((1 - half) * 512, 512), 512)] = other[...]
    else:
        out[...] = result


def side_attention(me, stats, remote, *shared, other):
    last = other is not None
    return pl.pallas_call(
        side_kernel,
        name="last_attention" if last else "side_attention",
        out_shape=jax.ShapeDtypeStruct((512, 1024 if last else 512), BF16),
        in_specs=smem(2) + vmem(len(shared) + 1 + last),
        out_specs=vmem(1)[0],
        scratch_shapes=[
            VM((4, 512, 128), BF16),
            VM((8, 80, 512), BF16),
            VM((512, 512), BF16),
        ],
        compiler_params=LIMIT,
        cost_estimate=cost(4 << 30, 6 << 20, 1 << 21),
    )(me, stats, remote, *shared, *([other] if last else []))


def pool_tables():
    pool = np.zeros((64, 64), np.float32)
    pick = np.zeros((64, 256), np.float32)
    for token in range(64):
        p = (token // 32) * 2 + token // 4 % 2
        q = (token // 16 % 2) * 2 + token // 2 % 2
        r = (token // 8 % 2) * 2 + token % 2
        for x in (2 * p, 2 * p + 1):
            for y in (2 * q, 2 * q + 1):
                pool[token, 8 * x + y] = 0.125
        pick[token, 64 * r : 64 * r + 64] = 1.0
    return jnp.asarray(pool, BF16), jnp.asarray(pick, F32)


def moved(array, by):
    size = lax.axis_size(AXES)
    pairs = [(i, i + by) for i in range(size) if 0 <= i + by < size]
    return lax.ppermute(array, AXES, pairs)


def swapped(array):
    size = lax.axis_size(AXES)
    return lax.ppermute(array, AXES, [(i, i ^ 1) for i in range(size)])


def crossed(array):
    size = lax.axis_size(AXES)
    pairs = [(i, (i - 1) % size if i % 2 == 0 else (i + 1) % size) for i in range(size)]
    return lax.ppermute(array, AXES, pairs)


def local(
    features, occupancy, neighbours, conv_weight, conv_bias, latent, token_proj, norm_gain,
    qkv_weight, out_weight,
):
    me = lax.axis_index(AXES)
    core = me % 2
    me_ref = me.astype(jnp.int32).reshape(1)
    xb, faces = prep(occupancy, features)
    back = moved(faces, 2)
    ahead = moved(faces, -2)
    partner = swapped(faces)
    relay = swapped(jnp.where(core == 1, back, ahead))
    conv_weight, faces_after = lax.optimization_barrier((conv_weight, faces))
    band, band_z, wv_t, wo_t, latent_t, proj_t = weights(
        conv_weight, qkv_weight, out_weight, latent, token_proj
    )
    bias = jnp.tile(conv_bias, 8)[None, :]
    acc = inner(xb, band)
    blocks, pooled, to_partner, to_cross = outer(
        neighbours, occupancy, me_ref, (faces, back, ahead, partner, relay), xb, acc, band, band_z,
        bias, latent, token_proj, norm_gain[None, :],
    )
    from_cross = crossed(to_cross)
    from_partner = swapped(to_partner)
    query, state, peak, stats = own_attention(
        occupancy, me_ref, to_partner, to_cross, qkv_weight, wv_t
    )
    conv_out = restore(blocks)
    shared = (query, state, peak, qkv_weight, wv_t, wo_t, latent_t, proj_t, pooled)
    first = side_attention(me_ref, stats, from_partner, *shared, other=None)
    tokens_out = side_attention(me_ref, stats, from_cross, *shared, other=first)
    return (conv_out, tokens_out)


def solution(mesh):
    return jax.shard_map(
        local,
        mesh=mesh,
        in_specs=(
            P(AXES, None, None),
            P(AXES),
            P(AXES, None),
            P(),
            P(),
            P(AXES, None),
            P(),
            P(),
            P(),
            P(),
        ),
        out_specs=(P(AXES, None, None), P(None, AXES)),
        check_vma=False,
    )
```

time: 111 us -> 88.9 us (0.80)
  Pallas kernels: 74.9 us -> 54.3 us
  waiting for transfers between devices: 2.35 us -> 15.2 us
  local copies, waits for them, and re-layouts: 14.1 us -> 6.2 us
  other arithmetic: 4.75 us -> 0.79 us
  starting transfers between devices: 13.4 us -> 10.1 us
    ppermute x2, waiting for transfers between devices: 2.34 us -> 15.2 us  [moved(): return lax.ppermute(array, AXES, pairs)]
    pallas_call x1, Pallas kernels: 15.4 us -> 9.55 us  [outer(): pl.pallas_call(outer_kernel, name='outer', out_shape=(jax.ShapeDtypeStruc...]
    pallas_call x2, Pallas kernels: 25.6 us -> 20 us  [side_attention(): pl.pallas_call(side_kernel, name='last_attention' if last else 'side_atte...]
    optimization_barrier x4 -> x0, local copies, waits for them, and re-layouts: 5.33 us -> none  [local(): lax.optimization_barrier((conv_weight, conv_bias, latent, token_proj, qkv...]
    ppermute x3, starting transfers between devices: 6.06 us -> 1.6 us  [swapped(): return lax.ppermute(array, AXES, [(i, i ^ 1) for i in range(size)])]
    unnamed x19 -> x33, local copies, waits for them, and re-layouts: 1.74 us -> 6.11 us
    select_n x2 -> x0, other arithmetic: 3.86 us -> none  [the longest x1 3.2 us: local(): jnp.where(has_peer, slot * count + peer % count, -1).reshape(-1)]
    transpose x3 -> x0, local copies, waits for them, and re-layouts: 3.27 us -> none  [the longest x1 1.75 us: bands(): taps = conv_weight.transpose(0, 2, 1).reshape(27 * 32, 32)]
  transfers between devices with their start and end apart: 6 -> 6, of which waited for: 1 -> 2; matrix products, arithmetic and copies ran while one was open for 16% -> 1% of each run, Pallas kernels for 39% -> 38%
where the time goes in v2:
time: 88.9 us; the launch traced here: 87.3 us
  Pallas kernels  54.3 us (61%)
  waiting for transfers between devices  15.2 us (17%)
  starting transfers between devices  10.1 us (11%)
  local copies, waits for them, and re-layouts  6.2 us (7%)
    pallas_call x2, Pallas kernels, side_attention(): pl.pallas_call(side_kernel, name='last_attention' if last else 'side_atte...  20 us
    pallas_call x1, Pallas kernels, own_attention(): pl.pallas_call(own_kernel, name='own_attention', out_shape=(jax.ShapeDtyp...  17.3 us
    ppermute x2, waiting for transfers between devices, moved(): return lax.ppermute(array, AXES, pairs)  15.2 us
    pallas_call x1, Pallas kernels, outer(): pl.pallas_call(outer_kernel, name='outer', out_shape=(jax.ShapeDtypeStruc...  9.55 us
    unnamed x33, local copies, waits for them, and re-layouts  6.11 us
    ppermute x2, starting transfers between devices, moved(): return lax.ppermute(array, AXES, pairs)  5.9 us
    ppermute x1, starting transfers between devices, crossed(): return lax.ppermute(array, AXES, pairs)  2.56 us
    pallas_call x1, Pallas kernels, weights(): pl.pallas_call(weights_kernel, name='weights', out_shape=(jax.ShapeDtypeS...  2.08 us
  transfers between devices with their start and end apart: 6, of which 2 were waited for; matrix products, arithmetic and copies ran while one was open for 1% of the time, Pallas kernels for 38%

profile of v2, /device:TPU:1, one launch (start us, length us, event | category | flops | bytes accessed | tf_op | source)
XLA Modules:
  0.0 87.3 jit_solution(11821197591383858886)
XLA Ops:
  0.6 0.0 copy-start
  0.6 0.0 copy-start.1
  0.7 1.1 %copy-done.1 = bf16[16,32,512]{2,1,0:T(8,128)(2,1)S(1)} copy-done((bf16[16,32,512]{2,1,0:T(8,128)(2,1)S(1)}, bf16[16,32,512]{2,1,0:T(8,128)(2,1)}, u32[]{:S(2)}) %copy-start.1) | copy-done | bytes 524312
  1.8 0.0 copy-start.2
  1.8 1.0 %copy-done.2 = bf16[512,512]{1,0:T(8,128)(2,1)S(1)} copy-done((bf16[512,512]{1,0:T(8,128)(2,1)S(1)}, bf16[512,512]{1,0:T(8,128)(2,1)}, u32[]{:S(2)}) %copy-start.2) | copy-done | bytes 524312
  2.8 0.0 copy-start.7
  2.8 0.7 copy-done.7
  3.5 0.0 copy-start.15
  3.5 0.0 copy-start.14
  3.5 0.0 copy-start.4
  3.5 0.0 copy-start.12
  3.5 1.5 %prep.1 = (f32[2,16,64,128]{3,2,1,0:T(8,128)S(1)}, bf16[96,8,256]{2,1,0:T(8,128)(2,1)S(1)}) custom-call(s32[16]{0:T(128)S(1)} %copy-done.7, bf16[16,32,512]{2,1,0:T(8,128)(2,1)S(1)} %copy-done.1, bf16[512,512]{1,0:T(8,128)(2,1)S(1)} %copy-done.2), custom_call_target="tpu_custom_call" | custom-call | flops 268435456 | bytes 2097152 | tf_op jit(solution)/shard_map/prep/pallas_call | solution.py:96
  5.0 1.3 %collective-permute-start.1 = (bf16[96,8,256]{2,1,0:T(8,128)(2,1)S(1)}, bf16[96,8,256]{2,1,0:T(8,128)(2,1)S(1)}, u32[]{:S(2)}, u32[]{:S(2)}) collective-permute-start(bf16[96,8,256]{2,1,0:T(8,128)(2,1)S(1)} %get-tuple-element.19.own), channel_id=1, source_target_pairs={{2,0},{3,1},{4,2},{5,3},{6,4},{7,5},{8,6},{9,7},{10,8},{11,9},{12,... | collective-permute-start | bytes 1179656 | tf_op jit(solution)/shard_map/ppermute | solution.py:725
  6.3 4.6 %collective-permute-start = (bf16[96,8,256]{2,1,0:T(8,128)(2,1)S(1)}, bf16[96,8,256]{2,1,0:T(8,128)(2,1)S(1)}, u32[]{:S(2)}, u32[]{:S(2)}) collective-permute-start(bf16[96,8,256]{2,1,0:T(8,128)(2,1)S(1)} %get-tuple-element.19.own), channel_id=1, source_target_pairs={{0,2},{1,3},{2,4},{3,5},{4,6},{5,7},{6,8},{7,9},{8,10},{9,11},{10,... | collective-permute-start | bytes 1179656 | tf_op jit(solution)/shard_map/ppermute | solution.py:725
  10.9 1.0 %collective-permute-start.2 = (bf16[96,8,256]{2,1,0:T(8,128)(2,1)S(1)}, bf16[96,8,256]{2,1,0:T(8,128)(2,1)}, u32[]{:S(2)}, u32[]{:S(2)}) collective-permute-start(bf16[96,8,256]{2,1,0:T(8,128)(2,1)S(1)} %get-tuple-element.19.own), channel_id=1, source_target_pairs={{0,1},{1,0},{2,3},{3,2},{4,5},{5,4},{6,7},{7,6},{8,9},{9,8},{10,11... | collective-permute-start | bytes 1179656 | tf_op jit(solution)/shard_map/ppermute | solution.py:730
  12.0 5.8 %collective-permute-done.1.ahead = bf16[96,8,256]{2,1,0:T(8,128)(2,1)S(1)} collective-permute-done((bf16[96,8,256]{2,1,0:T(8,128)(2,1)S(1)}, bf16[96,8,256]{2,1,0:T(8,128)(2,1)S(1)}, u32[]{:S(2)}, u32[]{:S(2)}) %collective-permute-start.1) | collective-permute-done | bytes 393248 | tf_op jit(solution)/shard_map/ppermute | solution.py:725
  17.8 9.3 %collective-permute-done.back = bf16[96,8,256]{2,1,0:T(8,128)(2,1)S(1)} collective-permute-done((bf16[96,8,256]{2,1,0:T(8,128)(2,1)S(1)}, bf16[96,8,256]{2,1,0:T(8,128)(2,1)S(1)}, u32[]{:S(2)}, u32[]{:S(2)}) %collective-permute-start) | collective-permute-done | bytes 393248 | tf_op jit(solution)/shard_map/ppermute | solution.py:725
  27.1 0.8 broadcast_select_fusion
  27.9 0.5 collective-permute-start.3
  28.4 0.0 copy-done.15
  28.4 0.1 broadcast_in_dim_tile.3.bias
  28.5 0.0 copy-done.14
  28.5 0.1 copy.16.neighbours
  28.6 0.0 copy-done
  28.6 0.0 copy-done.4
  28.6 0.0 copy-done.12
  28.6 0.0 copy-start.9
  28.6 1.4 %copy-done.9 = bf16[3,512,512]{2,1,0:T(8,128)(2,1)S(1)} copy-done((bf16[3,512,512]{2,1,0:T(8,128)(2,1)S(1)}, bf16[3,512,512]{2,1,0:T(8,128)(2,1)}, u32[]{:S(2)}) %copy-start.9) | copy-done | bytes 1572888
  30.0 0.0 copy-start.11
  30.0 1.0 %copy-done.11 = bf16[512,512]{1,0:T(8,128)(2,1)S(1)} copy-done((bf16[512,512]{1,0:T(8,128)(2,1)S(1)}, bf16[512,512]{1,0:T(8,128)(2,1)}, u32[]{:S(2)}) %copy-start.11) | copy-done | bytes 524312
  31.0 0.0 copy-start.13
  31.0 0.7 copy-done.13
  31.8 2.1 %weights.1 = (bf16[2304,256]{1,0:T(8,128)(2,1)S(1)}, bf16[768,256]{1,0:T(8,128)(2,1)S(1)}, bf16[512,512]{1,0:T(8,128)(2,1)S(1)}, bf16[512,512]{1,0:T(8,128)(2,1)...) custom-call(bf16[27,32,32]{2,1,0:T(8,128)(2,1)S(1)} %copy-done.12, bf16[32,256]{1,0:T(8,128)(2,1)S(1)} %copy-done.13, ...), custom_call_target="tpu_custom_call" | custom-call | flops 2147483648 | bytes 8388608 | tf_op jit(solution)/shard_map/weights/pallas_call | solution.py:185
  33.8 0.0 copy-start.3
  33.9 0.0 copy-start.5
  33.9 0.0 copy-start.6
  33.9 0.0 copy-start.8
  33.9 1.9 %inner.1.acc = f32[1024,256]{1,0:T(8,128)S(1)} custom-call(f32[2,16,64,128]{3,2,1,0:T(8,128)S(1)} %get-tuple-element.20.xb, bf16[2304,256]{1,0:T(8,128)(2,1)S(1)} %get-tuple-element.22.band), custom_call_target="tpu_custom_call" | custom-call | flops 1207959552 | bytes 4194304 | tf_op jit(solution)/shard_map/inner/pallas_call | solution.py:220
  35.8 0.0 collective-permute-done.2.partner
  35.8 0.0 collective-permute-done.3.relay
  35.8 0.0 copy-done.3
  35.9 0.0 copy-done.5
  35.9 0.0 copy-done.6
  35.9 0.0 copy-done.8
  35.9 0.0 copy-start.10
  35.9 9.6 %outer.1 = (f32[2,16,64,128]{3,2,1,0:T(8,128)S(1)}, bf16[1024,128]{1,0:T(8,128)(2,1)S(1)}, bf16[528,512]{1,0:T(8,128)(2,1)S(1)}, bf16[528,512]{1,0:T(8,128)(2,1)S(1)}) custom-call(s32[16,6]{1,0:T(8,128)S(1)} %copy.16.neighbours, s32[16]{0:T(128)S(1)} %copy-done.8, s32[1]{0:T(128)} %bitcast.me, bf16[96,8,256]{2,1,0:T(8,128)(2,1)S(1)} %get-tuple-element.19.own, ...), custom_call_target="tpu_custom_call" | custom-call | flops 1207959552 | bytes 8388608 | tf_op jit(solution)/shard_map/outer/pallas_call | solution.py:376
  45.5 0.1 collective-permute-start.5
  45.5 2.6 %collective-permute-start.4 = (bf16[528,512]{1,0:T(8,128)(2,1)S(1)}, bf16[528,512]{1,0:T(8,128)(2,1)S(1)}, u32[]{:S(2)}, u32[]{:S(2)}) collective-permute-start(bf16[528,512]{1,0:T(8,128)(2,1)S(1)} %get-tuple-element.26.to_cross), channel_id=1, source_target_pairs={{0,31},{1,2},{2,1},{3,4},{4,3},{5,6},{6,5},{7,8},{8,7},{9,10},{10,... | collective-permute-start | bytes 1622024 | tf_op jit(solution)/shard_map/ppermute | solution.py:736
  48.1 0.0 copy-done.10
  48.1 17.3 %own_attention.1 = (bf16[8,2,512,128]{3,2,1,0:T(8,128)(2,1)S(1)}, f32[8,2,72,512]{3,2,1,0:T(8,128)S(1)}, f32[8,2,8,512]{3,2,1,0:T(8,128)S(1)}, f32[8]{0:T(128)S(1)}) custom-call(s32[16]{0:T(128)S(1)} %copy-done.8, s32[1]{0:T(128)} %bitcast.me, bf16[528,512]{1,0:T(8,128)(2,1)S(1)} %get-tuple-element.25.to_partner, ...), custom_call_target="tpu_custom_call" | custom-call | flops 6442450944 | bytes 8388608 | tf_op jit(solution)/shard_map/own_attention/pallas_call | solution.py:591
  65.4 1.9 %restore.1 = bf16[16,32,512]{2,1,0:T(8,128)(2,1)} custom-call(f32[2,16,64,128]{3,2,1,0:T(8,128)S(1)} %get-tuple-element.24.blocks), custom_call_target="tpu_custom_call" | custom-call | flops 1048576 | bytes 2097152 | tf_op jit(solution)/shard_map/restore/pallas_call | solution.py:418
  67.3 0.0 collective-permute-done.5.remote
  67.3 9.6 %side_attention.1.rest_0_ = bf16[512,512]{1,0:T(8,128)(2,1)S(1)} custom-call(s32[1]{0:T(128)} %bitcast.me, f32[8]{0:T(128)S(1)} %get-tuple-element.28.stats, bf16[528,512]{1,0:T(8,128)(2,1)S(1)} %collective-permute-done.5.remote, bf16[8,2,512,128]{3,2,1,0:T(8,128)(2,1)S(1)} %get-tuple-element.29.query, f32[8,2,72,512]{3,2,1,0:T(8,128)S(1)} %get-tuple-element.30.state, ...), custom_call_target="tpu_custom_call" | custom-call | flops 4294967296 | bytes 6291456 | tf_op jit(solution)/shard_map/side_attention/pallas_call | solution.py:692
  76.9 0.0 collective-permute-done.4.remote
  76.9 10.4 %last_attention.1 = bf16[512,1024]{1,0:T(8,128)(2,1)} custom-call(s32[1]{0:T(128)} %bitcast.me, f32[8]{0:T(128)S(1)} %get-tuple-element.28.stats, bf16[528,512]{1,0:T(8,128)(2,1)S(1)} %collective-permute-done.4.remote, bf16[8,2,512,128]{3,2,1,0:T(8,128)(2,1)S(1)} %get-tuple-element.29.query, f32[8,2,72,512]{3,2,1,0:T(8,128)S(1)} %get-tuple-element.30.state, ...), custom_call_target="tpu_custom_call" | custom-call | flops 4294967296 | bytes 6291456 | tf_op jit(solution)/shard_map/last_attention/pallas_call | solution.py:692
  (1 shorter events, 0.0 us)
Async XLA Ops:
  0.6 27.9 %copy-start = (bf16[1024,512]{1,0:T(8,128)(2,1)S(1)}, bf16[1024,512]{1,0:T(8,128)(2,1)}, u32[]{:S(2)}) copy-start(bf16[1024,512]{1,0:T(8,128)(2,1)} %latent.3) | copy-start | bytes 3145732
  0.6 1.1 %copy-start.1 = (bf16[16,32,512]{2,1,0:T(8,128)(2,1)S(1)}, bf16[16,32,512]{2,1,0:T(8,128)(2,1)}, u32[]{:S(2)}) copy-start(bf16[16,32,512]{2,1,0:T(8,128)(2,1)} %feat.1) | copy-start | bytes 1572868
  1.8 1.0 %copy-start.2 = (bf16[512,512]{1,0:T(8,128)(2,1)S(1)}, bf16[512,512]{1,0:T(8,128)(2,1)}, u32[]{:S(2)}) copy-start(bf16[512,512]{1,0:T(8,128)(2,1)} %constant.33.clone.order) | copy-start | bytes 1572868
  2.8 0.7 copy-start.7
  3.5 24.9 %copy-start.15 = (f32[32]{0:T(128)S(1)}, f32[32]{0:T(128)}, u32[]{:S(2)}) copy-start(f32[32]{0:T(128)} %param.18) | copy-start | bytes 388
  3.5 25.0 %copy-start.14 = (s32[16,6]{0,1:T(8,128)S(1)}, s32[16,6]{0,1:T(8,128)}, u32[]{:S(2)}) copy-start(s32[16,6]{0,1:T(8,128)} %param.16) | copy-start | bytes 1156
  3.5 25.1 %copy-start.4 = (bf16[32,512]{1,0:T(8,128)(2,1)S(1)}, bf16[32,512]{1,0:T(8,128)(2,1)}, u32[]{:S(2)}) copy-start(bf16[32,512]{1,0:T(8,128)(2,1)} %proj.1) | copy-start | bytes 98308
  3.5 25.1 %copy-start.12 = (bf16[27,32,32]{2,1,0:T(8,128)(2,1)S(1)}, bf16[27,32,32]{2,1,0:T(8,128)(2,1)}, u32[]{:S(2)}) copy-start(bf16[27,32,32]{2,1,0:T(8,128)(2,1)} %conv) | copy-start | bytes 165892
  5.0 12.8 %collective-permute-start.1 = (bf16[96,8,256]{2,1,0:T(8,128)(2,1)S(1)}, bf16[96,8,256]{2,1,0:T(8,128)(2,1)S(1)}, u32[]{:S(2)}, u32[]{:S(2)}) collective-permute-start(bf16[96,8,256]{2,1,0:T(8,128)(2,1)S(1)} %get-tuple-element.19.own), channel_id=1, source_target_pairs={{2,0},{3,1},{4,2},{5,3},{6,4},{7,5},{8,6},{9,7},{10,8},{11,9},{12,... | collective-permute-start | bytes 1179656 | tf_op jit(solution)/shard_map/ppermute | solution.py:725
  6.3 20.8 %collective-permute-start = (bf16[96,8,256]{2,1,0:T(8,128)(2,1)S(1)}, bf16[96,8,256]{2,1,0:T(8,128)(2,1)S(1)}, u32[]{:S(2)}, u32[]{:S(2)}) collective-permute-start(bf16[96,8,256]{2,1,0:T(8,128)(2,1)S(1)} %get-tuple-element.19.own), channel_id=1, source_target_pairs={{0,2},{1,3},{2,4},{3,5},{4,6},{5,7},{6,8},{7,9},{8,10},{9,11},{10,... | collective-permute-start | bytes 1179656 | tf_op jit(solution)/shard_map/ppermute | solution.py:725
  10.9 24.9 %collective-permute-start.2 = (bf16[96,8,256]{2,1,0:T(8,128)(2,1)S(1)}, bf16[96,8,256]{2,1,0:T(8,128)(2,1)}, u32[]{:S(2)}, u32[]{:S(2)}) collective-permute-start(bf16[96,8,256]{2,1,0:T(8,128)(2,1)S(1)} %get-tuple-element.19.own), channel_id=1, source_target_pairs={{0,1},{1,0},{2,3},{3,2},{4,5},{5,4},{6,7},{7,6},{8,9},{9,8},{10,11... | collective-permute-start | bytes 1179656 | tf_op jit(solution)/shard_map/ppermute | solution.py:730
  27.9 7.9 %collective-permute-start.3 = (bf16[96,8,256]{2,1,0:T(8,128)(2,1)}, bf16[96,8,256]{2,1,0:T(8,128)(2,1)}, u32[]{:S(2)}, u32[]{:S(2)}) collective-permute-start(bf16[96,8,256]{2,1,0:T(8,128)(2,1)} %broadcast_select_fusion), channel_id=1, source_target_pairs={{0,1},{1,0},{2,3},{3,2},{4,5},{5,4},{6,7},{7,6},{8,9},{9,8},{10,11... | collective-permute-start | bytes 1179656 | tf_op jit(solution)/shard_map/ppermute | solution.py:730
  28.6 1.4 %copy-start.9 = (bf16[3,512,512]{2,1,0:T(8,128)(2,1)S(1)}, bf16[3,512,512]{2,1,0:T(8,128)(2,1)}, u32[]{:S(2)}) copy-start(bf16[3,512,512]{2,1,0:T(8,128)(2,1)} %qkv.7) | copy-start | bytes 4718596
  30.0 1.0 %copy-start.11 = (bf16[512,512]{1,0:T(8,128)(2,1)S(1)}, bf16[512,512]{1,0:T(8,128)(2,1)}, u32[]{:S(2)}) copy-start(bf16[512,512]{1,0:T(8,128)(2,1)} %out_weight.1) | copy-start | bytes 1572868
  31.0 0.7 copy-start.13
  33.8 2.0 %copy-start.3 = (f32[64,256]{1,0:T(8,128)S(1)}, f32[64,256]{1,0:T(8,128)}, u32[]{:S(2)}) copy-start(f32[64,256]{1,0:T(8,128)} %constant.36.clone.pick) | copy-start | bytes 196612
  33.9 2.0 %copy-start.5 = (bf16[64,64]{1,0:T(8,128)(2,1)S(1)}, bf16[64,64]{1,0:T(8,128)(2,1)}, u32[]{:S(2)}) copy-start(bf16[64,64]{1,0:T(8,128)(2,1)} %constant.35.clone.pool) | copy-start | bytes 24580
  33.9 2.0 %copy-start.6 = (f32[512]{0:T(512)S(1)}, f32[512]{0:T(512)}, u32[]{:S(2)}) copy-start(f32[512]{0:T(512)} %param.21) | copy-start | bytes 6148
  33.9 2.0 %copy-start.8 = (s32[16]{0:T(128)S(1)}, s32[16]{0:T(128)}, u32[]{:S(2)}) copy-start(s32[16]{0:T(128)} %occ.5) | copy-start | bytes 196
  35.9 12.2 %copy-start.10 = (bf16[3,512,512]{2,1,0:T(8,128)(2,1)S(1)}, bf16[3,512,512]{2,1,0:T(8,128)(2,1)}, u32[]{:S(2)}) copy-start(bf16[3,512,512]{2,1,0:T(8,128)(2,1)} %qkv.7) | copy-start | bytes 4718596
  45.5 21.8 %collective-permute-start.5 = (bf16[528,512]{1,0:T(8,128)(2,1)S(1)}, bf16[528,512]{1,0:T(8,128)(2,1)S(1)}, u32[]{:S(2)}, u32[]{:S(2)}) collective-permute-start(bf16[528,512]{1,0:T(8,128)(2,1)S(1)} %get-tuple-element.25.to_partner), channel_id=1, source_target_pairs={{0,1},{1,0},{2,3},{3,2},{4,5},{5,4},{6,7},{7,6},{8,9},{9,8},{10,11... | collective-permute-start | bytes 1622024 | tf_op jit(solution)/shard_map/ppermute | solution.py:730
  45.5 31.4 %collective-permute-start.4 = (bf16[528,512]{1,0:T(8,128)(2,1)S(1)}, bf16[528,512]{1,0:T(8,128)(2,1)S(1)}, u32[]{:S(2)}, u32[]{:S(2)}) collective-permute-start(bf16[528,512]{1,0:T(8,128)(2,1)S(1)} %get-tuple-element.26.to_cross), channel_id=1, source_target_pairs={{0,31},{1,2},{2,1},{3,4},{4,3},{5,6},{6,5},{7,8},{8,7},{9,10},{10,... | collective-permute-start | bytes 1622024 | tf_op jit(solution)/shard_map/ppermute | solution.py:736
